TPU v7x, 32 devices: a whole 2x2x4 slice. The times are simulated.
32 devices in a mesh: outer: 8 (over z, x), inner: 4 (over y, core).
Axes of the slice: x: 2, y: 2, z: 4, core: 2. Of those that a mesh axis runs over, the one named last changes fastest.
Arguments:
- resid: bfloat16 [4096, 2048], P(('outer', 'inner')), may hold values from -40 to 40
- queries: bfloat16 [4096, 256], P(('outer', 'inner')), may hold values from -80 to 80
- keyvals: bfloat16 [4096, 256], P(('outer', 'inner')), may hold values from -10 to 10
- piece_order: int32 [8], replicated, may hold values from 0 to 7, each once
- out_proj: bfloat16 [256, 2048], replicated, may hold values from -0.75 to 0.75
- mlp_gain: float32 [2048], replicated, may hold values from 0.25 to 1.75
- w_gate: bfloat16 [2048, 7168], P('inner', 'outer'), may hold values from -0.125 to 0.125
- w_up: bfloat16 [2048, 7168], P('inner', 'outer'), may hold values from -0.125 to 0.125
- w_down: bfloat16 [7168, 2048], P('outer', 'inner'), may hold values from -0.0625 to 0.0625
Outputs:
- layer_out: bfloat16 [4096, 2048], P(('outer', 'inner'))
Inputs may be any that keep to these rules, and one draw needn't show every extreme that they name: `piece_order`: each of the 8 piece numbers appears once.
All inputs are finite; a program needn't handle non-finite values.
Results may differ from a plain program's by a relative error of at most 0.014.
Values may be sent and summed in bfloat16 or wider, within the bound.
A program may use at most 64 MiB of HBM per device.

v0:
```python
import functools

import jax
import jax.numpy as jnp
from jax import lax
from jax.experimental import pallas as pl
from jax.experimental.pallas import tpu as pltpu
from jax.sharding import PartitionSpec as P

MESH = pl.DeviceIdType.MESH
F32 = jnp.float32
BF16 = jnp.bfloat16
EPS = 1e-05


def layer_kernel(
    n_out, n_in,
    order_ref, resid_ref, query_ref, kv_ref, proj_ref, gain_ref, wg_ref, wu_ref, wd_ref,
    out_ref,
    kv_all, wg, wu, wd, tok, after, hidden, x_out, x_in, own_part, z_out, z_in,
    kv_loc, kv_snd, kv_relay_snd, kv_rcv, w_loc, w_pair_snd, w_snd, w_relay_snd, w_rcv,
    z_snd, z_rcv, g_snd, g_rcv, x_snd, x_rcv, rx_snd, rx_rcv, rz_snd, rz_rcv,
):
    o = lax.axis_index("outer")
    i = lax.axis_index("inner")
    nz = n_out // 2
    z, x = o // 2, o % 2
    core = i % 2
    x_peer = (z * 2 + 1 - x, i)
    core_peer = (o, i + 1 - 2 * core)
    rows = resid_ref.shape[0]
    head = kv_ref.shape[1] // 2
    heads = query_ref.shape[1] // head
    pieces = order_ref.shape[0]
    block = n_in * rows
    span = block // pieces
    depth = wg_ref.shape[0]

    def remote(src, dst, ssem, rsem, device):
        return pltpu.make_async_remote_copy(
            src_ref=src, dst_ref=dst, send_sem=ssem, recv_sem=rsem,
            device_id=device, device_id_type=MESH,
        )

    barrier = pltpu.get_barrier_semaphore()
    after_o, before_o = lax.rem(o + 1, n_out), lax.rem(o + n_out - 1, n_out)
    count = 0
    for d in range(1, n_in):
        pl.semaphore_signal(barrier, inc=1, device_id=(o, lax.rem(i + d, n_in)), device_id_type=MESH)
        count += 1
    for d in range(n_in // 2):
        for there in (after_o, before_o):
            pl.semaphore_signal(
                barrier, inc=1, device_id=(there, lax.rem(i + 2 * d, n_in)), device_id_type=MESH)
            count += 1
    for d in range(1, nz):
        pl.semaphore_signal(
            barrier, inc=1, device_id=(lax.rem(z + d, nz) * 2 + x, i), device_id_type=MESH)
        count += 1
    pl.semaphore_signal(barrier, inc=1, device_id=x_peer, device_id_type=MESH)
    count += 1
    pl.semaphore_wait(barrier, count)

    own_rows = pl.ds(pl.multiple_of(i * rows, rows), rows)
    kv_copy = pltpu.make_async_copy(kv_ref, kv_all.at[own_rows], kv_loc)
    kv_copy.start()

    steps = range(1, n_in // 2)

    def kv_slot(part, q):
        return kv_all.at[pl.ds(pl.multiple_of(part * block + q * rows, rows), rows)]

    def kv_send(part, d):
        return remote(kv_ref, kv_slot(part, i), kv_snd.at[part, d], kv_rcv.at[part, i],
                      (after_o if part else o, lax.rem(i + 2 * d, n_in)))

    def kv_relay(part, d):
        q = lax.rem(i + n_in - 2 * d, n_in)
        src = kv_ref if part == 0 and d == 0 else kv_slot(part, q)
        return remote(src, kv_slot(part, q), kv_relay_snd.at[part, d], kv_rcv.at[part, q], core_peer)

    def kv_arrived(part, q):
        here = kv_slot(part, q)
        remote(here, here, kv_relay_snd.at[part, 0], kv_rcv.at[part, q], core_peer).wait_recv()

    for d in steps:
        kv_send(0, d).start()

    @pl.when(o < n_out - 1)
    def _():
        for d in range(n_in // 2):
            kv_send(1, d).start()

    kv_relay(0, 0).start()

    def slot(k, q):
        if k == 2:
            return wd.at[q]
        full = wg if k == 0 else wu
        return full.at[pl.ds(pl.multiple_of(q * depth, depth), depth)]

    srcs = (wg_ref, wu_ref, wd_ref)
    def w_far(k, d):
        return remote(srcs[k], slot(k, i), w_snd.at[k, d], w_rcv.at[k, i],
                      (o, lax.rem(i + 2 * d, n_in)))

    def w_pair(k):
        return remote(srcs[k], slot(k, i), w_pair_snd.at[k], w_rcv.at[k, i], core_peer)

    def w_arrived(k, q):
        remote(slot(k, q), slot(k, q), w_pair_snd.at[k], w_rcv.at[k, q], core_peer).wait_recv()

    def w_relay(k, d):
        q = lax.rem(i + n_in - 2 * d, n_in)
        return remote(slot(k, q), slot(k, q), w_relay_snd.at[k, d], w_rcv.at[k, q], core_peer)

    def w_local(k):
        return pltpu.make_async_copy(srcs[k], slot(k, i), w_loc.at[k])

    for k in range(3):
        for d in steps:
            w_far(k, d).start()
    for k in range(3):
        w_pair(k).start()
        w_local(k).start()

    def relay_weight(k):
        for d in steps:
            w_arrived(k, lax.rem(i + n_in - 2 * d, n_in))
            w_relay(k, d).start()

    def weight_ready(k):
        w_local(k).wait()
        for d in range(n_in // 2):
            w_arrived(k, lax.rem(partner + 2 * d, n_in))

    lane = lax.broadcasted_iota(jnp.int32, (rows, block), 1)
    key_pos = jnp.zeros((rows, block), jnp.int32)
    for p in range(pieces):
        key_pos = jnp.where(lane // span == p, order_ref[p] * span + lane % span, key_pos)
    row = lax.broadcasted_iota(jnp.int32, (rows, block), 0)
    query_pos = jnp.zeros((rows, block), jnp.int32)
    for p in range(rows // span):
        query_pos = jnp.where(
            row // span == p, order_ref[i * (rows // span) + p] * span + row % span, query_pos)
    own_visible = key_pos <= query_pos
    before_visible = (jnp.zeros((rows, block), jnp.int32) + o) > 0

    @pl.when(o == 0)
    def _():
        kv_all[block:, :] = jnp.zeros((block, 2 * head), BF16)

    for d in steps:
        kv_arrived(0, lax.rem(i + n_in - 2 * d, n_in))
        kv_relay(0, d).start()

    @pl.when(o > 0)
    def _():
        for d in range(n_in // 2):
            kv_arrived(1, lax.rem(i + n_in - 2 * d, n_in))
            kv_relay(1, d).start()

    partner = i + 1 - 2 * core
    kv_copy.wait()
    for d in range(n_in // 2):
        kv_arrived(0, lax.rem(partner + 2 * d, n_in))

    @pl.when(o > 0)
    def _():
        for d in range(n_in // 2):
            kv_arrived(1, lax.rem(partner + 2 * d, n_in))

    parts = []
    nt = (((1,), (1,)), ((), ()))
    for h in range(heads):
        query = query_ref[:, h * head:(h + 1) * head]
        own_score = lax.dot_general(
            query, kv_all[:block, :head], nt, preferred_element_type=F32) * head ** (-0.5)
        before_score = lax.dot_general(
            query, kv_all[block:, :head], nt, preferred_element_type=F32) * head ** (-0.5)
        own_score = jnp.where(own_visible, own_score, -1e30)
        before_score = jnp.where(before_visible, before_score, -1e30)
        top = jnp.maximum(
            jnp.max(own_score, axis=1, keepdims=True), jnp.max(before_score, axis=1, keepdims=True))
        own_w = jnp.where(own_visible, jnp.exp(own_score - top), 0.0)
        before_w = jnp.where(before_visible, jnp.exp(before_score - top), 0.0)
        total = jnp.sum(own_w, axis=1, keepdims=True) + jnp.sum(before_w, axis=1, keepdims=True)
        mixed = jnp.dot(own_w.astype(BF16), kv_all[:block, head:], preferred_element_type=F32)
        mixed += jnp.dot(before_w.astype(BF16), kv_all[block:, head:], preferred_element_type=F32)
        parts.append((mixed / total).astype(BF16))
    attended = jnp.concatenate(parts, axis=1)
    after_attn = (
        resid_ref[...].astype(F32) + jnp.dot(attended, proj_ref[...], preferred_element_type=F32)
    ).astype(BF16)
    after[...] = after_attn
    wide = after_attn.astype(F32)
    normed = wide * lax.rsqrt(jnp.mean(wide * wide, axis=1, keepdims=True) + EPS) * gain_ref[...]

    def tok_rows(zz, xx):
        return tok.at[pl.ds(pl.multiple_of((zz * 2 + xx) * rows, rows), rows)]

    tok_rows(z, x)[...] = normed.astype(BF16)

    def z_device(zz):
        return (zz * 2 + x, i)

    def inside(zz):
        return jnp.logical_and(zz >= 0, zz < nz)

    def tok_z(way, h):
        step = 1 - 2 * way
        here = tok_rows(z - step * h, x)
        return remote(here, here, z_snd.at[way, h], z_rcv.at[way, h], z_device(z + step))

    def tok_z_arrived(way, h):
        here = tok_rows(z - (1 - 2 * way) * (h + 1), x)
        remote(here, here, z_snd.at[way, h], z_rcv.at[way, h], x_peer).wait_recv()

    keep = rows - rows // 4

    def tok_x_own(xx):
        here = tok_rows(z, xx)
        return remote(here, here, x_snd.at[z], x_rcv.at[z], x_peer)

    def tok_first(zz, xx):
        here = tok.at[pl.ds(pl.multiple_of((zz * 2 + xx) * rows, rows), keep)]
        return remote(here, here, x_snd.at[zz], x_rcv.at[zz], x_peer)

    def tok_last(way, h, hops, to):
        zz = z - (1 - 2 * way) * hops
        here = tok.at[pl.ds(pl.multiple_of((zz * 2 + 1 - x) * rows + keep, rows // 4), rows - keep)]
        return remote(here, here, g_snd.at[way, h], g_rcv.at[way, h], to)

    def last_hop(h):
        for way in range(2):
            step = 1 - 2 * way

            @pl.when(jnp.logical_and(inside(z - step * h), inside(z + step)))
            def _():
                tok_last(way, h, h, z_device(z + step)).start()

    def last_arrived(h):
        for way in range(2):
            @pl.when(inside(z - (1 - 2 * way) * (h + 1)))
            def _():
                tok_last(way, h, h + 1, x_peer).wait_recv()

    for way in range(2):
        @pl.when(inside(z + 1 - 2 * way))
        def _():
            tok_z(way, 0).start()
    tok_x_own(x).start()
    for h in range(nz - 1):
        for way in range(2):
            step = 1 - 2 * way
            source = z - step * (h + 1)

            @pl.when(inside(source))
            def _():
                tok_z_arrived(way, h)

                @pl.when(inside(z + step))
                def _():
                    tok_z(way, h + 1).start()

                tok_first(source, x).start()
        if h == 0:
            tok_x_own(1 - x).wait_recv()
        else:
            last_arrived(h - 1)
        last_hop(h)
        if h < 2:
            relay_weight(h)
    for k in range(min(nz - 1, 2), 2):
        relay_weight(k)
    weight_ready(0)
    weight_ready(1)

    chunks = n_in // 2
    width = wd_ref.shape[1]

    def columns_of(p):
        return lax.rem(i // 2 + chunks - p, chunks)

    def sum_x(p, zz):
        return remote(x_out.at[p, zz], x_in.at[p, zz], rx_snd.at[p, zz], rx_rcv.at[p, zz], x_peer)

    def sum_z(p, way, zz):
        step = jnp.where(inside(z + 1 - 2 * way), 1 - 2 * way, 0)
        return remote(z_out.at[p, zz], z_in.at[p, way, zz], rz_snd.at[p, zz], rz_rcv.at[p, way, zz],
                      z_device(z + step))

    def down(p, zz):
        def half(xx):
            return hidden[pl.ds(pl.multiple_of((zz * 2 + xx) * rows, rows), rows), :]

        both = jnp.concatenate([half(1 - x), half(x)], axis=0)
        for q in range(2):
            part = jnp.dot(both, wd[2 * columns_of(p) + q], preferred_element_type=F32)
            x_out[p, zz, :, q * width:(q + 1) * width] = part[:rows].astype(BF16)
            own_part[p, zz, :, q * width:(q + 1) * width] = part[rows:]
        sum_x(p, zz).start()

    def owner(j):
        way = j % 2
        return way, z + (nz - 1 - j // 2) * (1 - 2 * way)

    def finish(p, j):
        way, zz = owner(j)
        more = inside(z - (1 - 2 * way))

        @pl.when(inside(zz))
        def _():
            sum_x(p, zz).wait_recv()

            @pl.when(more)
            def _():
                sum_z(p, way, zz).wait_recv()
                z_out[p, zz] = (
                    own_part[p, zz] + x_in[p, zz].astype(F32) + z_in[p, way, zz].astype(F32)
                ).astype(BF16)

            @pl.when(jnp.logical_not(more))
            def _():
                z_out[p, zz] = (own_part[p, zz] + x_in[p, zz].astype(F32)).astype(BF16)

            sum_z(p, way, zz).start()

    w_local(2).wait()
    w_arrived(2, partner)

    def hidden_step(j, carry):
        zz = z + ((j + 1) // 2) * (1 - 2 * (j % 2))

        @pl.when(inside(zz))
        def _():
            @pl.when(j > 0)
            def _():
                tok_first(zz, 1 - x).wait_recv()

            @pl.when((j + 1) // 2 == nz - 1)
            def _():
                tok_last(1 - j % 2, nz - 2, nz - 1, x_peer).wait_recv()

            here = pl.ds(pl.multiple_of(zz * 2 * rows, 2 * rows), 2 * rows)
            tokens = tok[here, :]
            gate = jnp.dot(tokens, wg[...], preferred_element_type=F32)
            upward = jnp.dot(tokens, wu[...], preferred_element_type=F32)
            hidden[here, :] = (gate / (1.0 + jnp.exp(-gate)) * upward).astype(BF16)

            @pl.when(j == 0)
            def _():
                down(0, zz)

        return carry

    lax.fori_loop(0, 2 * nz - 1, hidden_step, 0)

    def down_first(j, carry):
        _, zz = owner(j)

        @pl.when(inside(zz))
        def _():
            down(0, zz)

        return carry

    lax.fori_loop(0, 2 * (nz - 1), down_first, 0)
    relay_weight(2)
    for d in range(1, n_in // 2):
        w_arrived(2, lax.rem(partner + 2 * d, n_in))

    def finish_first(j, carry):
        finish(0, j)
        return carry

    lax.fori_loop(0, 2, finish_first, 0)
    turns = 2 * nz - 1

    def down_rest(j, carry):
        _, zz = owner(j % turns)

        @pl.when(inside(zz))
        def _():
            down(1 + j // turns, zz)

        return carry

    lax.fori_loop(0, (chunks - 1) * turns, down_rest, 0)
    lax.fori_loop(2, turns - 1, finish_first, 0)

    def finish_rest(j, carry):
        finish(1 + j // (turns - 1), j % (turns - 1))
        return carry

    lax.fori_loop(0, (chunks - 1) * (turns - 1), finish_rest, 0)
    for p in range(chunks):
        here = pl.ds(pl.multiple_of(columns_of(p) * 2 * width, 2 * width), 2 * width)
        for way in range(2):
            @pl.when(inside(z - (1 - 2 * way)))
            def _():
                sum_z(p, way, z).wait_recv()
                own_part[p, z] = own_part[p, z] + z_in[p, way, z].astype(F32)
        sum_x(p, z).wait_recv()
        out_ref[:, here] = (
            after[:, here].astype(F32) + (own_part[p, z] + x_in[p, z].astype(F32))).astype(BF16)

    for d in steps:
        kv_send(0, d).wait_send()
    for d in range(n_in // 2):
        kv_relay(0, d).wait_send()

    @pl.when(o < n_out - 1)
    def _():
        for d in range(n_in // 2):
            kv_send(1, d).wait_send()

    @pl.when(o > 0)
    def _():
        for d in range(n_in // 2):
            kv_relay(1, d).wait_send()

    for k in range(3):
        w_pair(k).wait_send()
        for d in steps:
            w_far(k, d).wait_send()
            w_relay(k, d).wait_send()
    for h in range(nz - 1):
        for way in range(2):
            step = 1 - 2 * way

            @pl.when(jnp.logical_and(inside(z - step * h), inside(z + step)))
            def _():
                tok_z(way, h).wait_send()
                tok_last(way, h, h, x_peer).wait_send()
    for zz in range(nz):
        @pl.when(z == zz)
        def _():
            tok_x_own(x).wait_send()

        @pl.when(z != zz)
        def _():
            tok_first(zz, x).wait_send()

        for p in range(chunks):
            sum_x(p, zz).wait_send()

            @pl.when(z != zz)
            def _():
                sum_z(p, 0, zz).wait_send()


def per_device(n_out, n_in, resid, queries, keyvals, piece_order, out_proj, mlp_gain, w_gate, w_up, w_down):
    rows, model = resid.shape
    units = w_gate.shape[1]
    nz, chunks = n_out // 2, n_in // 2
    dma = pltpu.SemaphoreType.DMA
    vmem = pl.BlockSpec(memory_space=pltpu.VMEM)
    hbm = pl.BlockSpec(memory_space=pl.ANY)
    return pl.pallas_call(
        functools.partial(layer_kernel, n_out, n_in),
        out_shape=jax.ShapeDtypeStruct(resid.shape, BF16),
        in_specs=[pl.BlockSpec(memory_space=pltpu.SMEM)] + [vmem] * 5 + [hbm] * 3,
        out_specs=vmem,
        scratch_shapes=[
            pltpu.VMEM((2 * n_in * rows, keyvals.shape[1]), BF16),
            pltpu.VMEM((model, units), BF16),
            pltpu.VMEM((model, units), BF16),
            pltpu.VMEM((n_in,) + w_down.shape, BF16),
            pltpu.VMEM((n_out * rows, model), BF16),
            pltpu.VMEM((rows, model), BF16),
            pltpu.VMEM((n_out * rows, units), BF16),
            pltpu.VMEM((chunks, nz, rows, model // chunks), BF16),
            pltpu.VMEM((chunks, nz, rows, model // chunks), BF16),
            pltpu.VMEM((chunks, nz, rows, model // chunks), F32),
            pltpu.VMEM((chunks, nz, rows, model // chunks), BF16),
            pltpu.VMEM((chunks, 2, nz, rows, model // chunks), BF16),
            dma(()), dma((2, n_in)), dma((2, n_in)), dma((2, n_in)),
            dma((3,)), dma((3,)), dma((3, n_in)), dma((3, n_in)), dma((3, n_in)),
            dma((2, nz)), dma((2, nz)), dma((2, nz)), dma((2, nz)), dma((nz,)), dma((nz,)),
            dma((chunks, nz)), dma((chunks, nz)), dma((chunks, nz)), dma((chunks, 2, nz)),
        ],
        compiler_params=pltpu.CompilerParams(
            collective_id=0, has_side_effects=True, vmem_limit_bytes=60000 * 1024
        ),
        name="layer",
    )(piece_order, resid, queries, keyvals, out_proj, mlp_gain.reshape(1, -1), w_gate, w_up, w_down)


def solution(mesh):
    placed = (
        P(("outer", "inner"), None),
        P(("outer", "inner"), None),
        P(("outer", "inner"), None),
        P(),
        P(),
        P(),
        P("inner", "outer"),
        P("inner", "outer"),
        P("outer", "inner"),
    )
    return jax.shard_map(
        functools.partial(per_device, mesh.shape["outer"], mesh.shape["inner"]),
        mesh=mesh,
        in_specs=placed,
        out_specs=P(("outer", "inner"), None),
        check_vma=False,
    )
```

profile of v0, /device:TPU:0, one launch (start us, length us, event | category | flops | bytes accessed | tf_op | source)
XLA Modules:
  0.0 117.6 jit_solution(9330473844844526908)
XLA Ops:
  0.0 115.7 %layer.1 = bf16[128,2048]{1,0:T(8,128)(2,1)} custom-call(s32[8]{0:T(128)} %order_ref.1, bf16[128,2048]{1,0:T(8,128)(2,1)} %resid_ref.1, bf16[128,256]{1,0:T(8,128)(2,1)} %query_ref.1, bf16[128,256]{1,0:T(8,128)(2,1)} %kv_ref.1, bf16[256,2048]{1,0:T(8,128)(2,1)} %proj_ref.1, f32[1,2048]{1,0:T(1,128)} %bitcast.1, bf16[512,896]{1,0:T(8,128)(2,1)} %wg_ref.1, ...), custom_call_target="tpu_custom_call" | custom-call | tf_op jit(solution)/shard_map/layer/pallas_call | solution.py:460
  115.7 1.9 %copy.11 = bf16[128,2048]{1,0:T(8,128)(2,1)} copy(bf16[128,2048]{1,0:T(8,128)(2,1)} %layer.1) | data formatting | bytes 1048576
where the time goes:
time: 118 us
  Pallas kernels  116 us (98%)
  local copies, waits for them, and re-layouts  1.88 us (2%)
    pallas_call x1, Pallas kernels, per_device(): pl.pallas_call(functools.partial(layer_kernel, n_out, n_in), out_shape=ja...  116 us

commit v1 on v0

v1 whole, which is shorter than its diff:
```python
import functools

import jax
import jax.numpy as jnp
from jax import lax
from jax.experimental import pallas as pl
from jax.experimental.pallas import tpu as pltpu
from jax.sharding import PartitionSpec as P

MESH = pl.DeviceIdType.MESH
F32 = jnp.float32
BF16 = jnp.bfloat16
EPS = 1e-05


def layer_kernel(
    n_out, n_in, cuts, pieces_w, early,
    order_ref, resid_ref, query_ref, kv_ref, proj_ref, gain_ref, wg_ref, wu_ref, wd_ref,
    out_ref,
    kv_all, wg, wu, wd, tok, after, att_own, res_in, att_in, gates, hidden,
    x_out, x_in, own_part, z_out, z_in, h_own, h_out, h_in,
    kv_loc, kv_snd, kv_relay_snd, kv_rcv, w_loc, w_pair_snd, w_snd, w_relay_snd, w_rcv,
    r_snd, r_rcv, a_snd, a_rcv, n_snd, n_rcv, z_snd, z_rcv, g_snd, g_rcv, x_snd, x_rcv,
    rx_snd, rx_rcv, rz_snd, rz_rcv, rh_snd, rh_rcv,
):
    o = lax.axis_index("outer")
    i = lax.axis_index("inner")
    nz = n_out // 2
    z, x = o // 2, o % 2
    core = i % 2
    partner = i + 1 - 2 * core
    x_peer = (z * 2 + 1 - x, i)
    core_peer = (o, partner)
    rows = resid_ref.shape[0]
    head = kv_ref.shape[1] // 2
    heads = query_ref.shape[1] // head
    pieces = order_ref.shape[0]
    block = n_in * rows
    span = block // pieces
    depth = wg_ref.shape[0]
    units, width = wd_ref.shape
    chips = n_in // 2
    parts_n = chips * cuts
    cw = width // cuts
    keep = rows // 2
    last_z = nz - 1

    def remote(src, dst, ssem, rsem, device):
        return pltpu.make_async_remote_copy(
            src_ref=src, dst_ref=dst, send_sem=ssem, recv_sem=rsem,
            device_id=device, device_id_type=MESH,
        )

    def inside(zz):
        return jnp.logical_and(zz >= 0, zz < nz)

    def middle(zz):
        return jnp.logical_and(zz > 0, zz < last_z)

    def z_device(zz):
        return (zz * 2 + x, i)

    barrier = pltpu.get_barrier_semaphore()
    after_o, before_o = lax.rem(o + 1, n_out), lax.rem(o + n_out - 1, n_out)
    count = 0
    for d in range(1, n_in):
        pl.semaphore_signal(barrier, inc=1, device_id=(o, lax.rem(i + d, n_in)), device_id_type=MESH)
        count += 1
    for d in range(n_in // 2):
        for there in (after_o, before_o):
            pl.semaphore_signal(
                barrier, inc=1, device_id=(there, lax.rem(i + 2 * d, n_in)), device_id_type=MESH)
            count += 1
    for d in range(1, nz):
        pl.semaphore_signal(
            barrier, inc=1, device_id=(lax.rem(z + d, nz) * 2 + x, i), device_id_type=MESH)
        count += 1
    pl.semaphore_signal(barrier, inc=1, device_id=x_peer, device_id_type=MESH)
    count += 1
    pl.semaphore_wait(barrier, count)

    own_rows = pl.ds(pl.multiple_of(i * rows, rows), rows)
    kv_copy = pltpu.make_async_copy(kv_ref, kv_all.at[own_rows], kv_loc)
    kv_copy.start()

    steps = range(1, chips)

    def kv_slot(part, q):
        return kv_all.at[pl.ds(pl.multiple_of(part * block + q * rows, rows), rows)]

    def kv_send(part, d):
        return remote(kv_ref, kv_slot(part, i), kv_snd.at[part, d], kv_rcv.at[part, i],
                      (after_o if part else o, lax.rem(i + 2 * d, n_in)))

    def kv_relay(part, d):
        q = lax.rem(i + n_in - 2 * d, n_in)
        src = kv_ref if part == 0 and d == 0 else kv_slot(part, q)
        return remote(src, kv_slot(part, q), kv_relay_snd.at[part, d], kv_rcv.at[part, q], core_peer)

    def kv_arrived(part, q):
        here = kv_slot(part, q)
        remote(here, here, kv_relay_snd.at[part, 0], kv_rcv.at[part, q], core_peer).wait_recv()

    for d in steps:
        kv_send(0, d).start()

    @pl.when(o < n_out - 1)
    def _():
        for d in range(chips):
            kv_send(1, d).start()

    kv_relay(0, 0).start()

    def tok_rows(zz, xx, start=0, size=rows):
        return tok.at[pl.ds(pl.multiple_of((zz * 2 + xx) * rows + start, 16), size)]

    targets = (z_device(z + 1), z_device(z - 1), x_peer)
    sources = ((z - 1, x), (z + 1, x), (z, 1 - x))

    def first_resid(link):
        return remote(resid_ref.at[pl.ds(0, early)], res_in.at[link], r_snd.at[link], r_rcv.at[link],
                      targets[link])

    def first_attended(link):
        return remote(att_own.at[pl.ds(0, early)], att_in.at[link], a_snd.at[link], a_rcv.at[link],
                      targets[link])

    def first_normed(link, source=None):
        here = tok_rows(*(source or (z, x)), early, rows - early)
        return remote(here, here, n_snd.at[link], n_rcv.at[link], targets[link])

    def send_link(link, act):
        if link == 2:
            act()
        else:
            pl.when(inside(z + 1 - 2 * link))(act)

    for link in range(3):
        send_link(link, lambda link=link: first_resid(link).start())

    def slot(k, q, s):
        if k == 2:
            return wd.at[q, s]
        full = wg if k == 0 else wu
        size = depth // pieces_w
        return full.at[pl.ds(pl.multiple_of(q * depth + s * size, size), size)]

    srcs = (wg_ref, wu_ref, wd_ref)

    def w_src(k, s):
        if k == 2:
            return wd_ref.at[:, pl.ds(s * cw, cw)]
        size = depth // pieces_w
        return srcs[k].at[pl.ds(s * size, size)]

    def w_parts(k):
        return cuts if k == 2 else pieces_w

    def w_far(k, d, s):
        return remote(w_src(k, s), slot(k, i, s), w_snd.at[k, d, s], w_rcv.at[k, i, s],
                      (o, lax.rem(i + 2 * d, n_in)))

    def w_pair(k, s):
        return remote(w_src(k, s), slot(k, i, s), w_pair_snd.at[k, s], w_rcv.at[k, i, s], core_peer)

    def w_arrived(k, q, s):
        here = slot(k, q, s)
        remote(here, here, w_pair_snd.at[k, s], w_rcv.at[k, q, s], core_peer).wait_recv()

    def w_relay(k, d, s):
        q = lax.rem(i + n_in - 2 * d, n_in)
        here = slot(k, q, s)
        return remote(here, here, w_relay_snd.at[k, d, s], w_rcv.at[k, q, s], core_peer)

    def w_local(k, s):
        return pltpu.make_async_copy(w_src(k, s), slot(k, i, s), w_loc.at[k, s])

    for k in range(3):
        for s in range(w_parts(k)):
            for d in steps:
                w_far(k, d, s).start()
    for k in range(3):
        for s in range(w_parts(k)):
            w_pair(k, s).start()
            w_local(k, s).start()

    def relay_weight(k, s):
        for d in steps:
            w_arrived(k, lax.rem(i + n_in - 2 * d, n_in), s)
            w_relay(k, d, s).start()

    def weight_ready(k):
        for s in range(w_parts(k)):
            w_local(k, s).wait()
            for d in range(chips):
                w_arrived(k, lax.rem(partner + 2 * d, n_in), s)

    lane = lax.broadcasted_iota(jnp.int32, (rows, block), 1)
    key_pos = jnp.zeros((rows, block), jnp.int32)
    for p in range(pieces):
        key_pos = jnp.where(lane // span == p, order_ref[p] * span + lane % span, key_pos)
    row = lax.broadcasted_iota(jnp.int32, (rows, block), 0)
    query_pos = jnp.zeros((rows, block), jnp.int32)
    for p in range(rows // span):
        query_pos = jnp.where(
            row // span == p, order_ref[i * (rows // span) + p] * span + row % span, query_pos)
    own_visible = key_pos <= query_pos
    before_visible = (jnp.zeros((rows, block), jnp.int32) + o) > 0

    @pl.when(o == 0)
    def _():
        kv_all[block:, :] = jnp.zeros((block, 2 * head), BF16)

    for zz in (0, last_z):
        @pl.when(z != zz)
        def _():
            x_in[:, zz, keep:, :] = jnp.zeros((parts_n, rows - keep, 2 * cw), BF16)

    for d in steps:
        kv_arrived(0, lax.rem(i + n_in - 2 * d, n_in))
        kv_relay(0, d).start()

    @pl.when(o > 0)
    def _():
        for d in range(chips):
            kv_arrived(1, lax.rem(i + n_in - 2 * d, n_in))
            kv_relay(1, d).start()

    kv_copy.wait()
    for d in range(chips):
        kv_arrived(0, lax.rem(partner + 2 * d, n_in))

    @pl.when(o > 0)
    def _():
        for d in range(chips):
            kv_arrived(1, lax.rem(partner + 2 * d, n_in))

    if True:
        parts = []
        nt = (((1,), (1,)), ((), ()))
        for h in range(heads):
            query = query_ref[:, h * head:(h + 1) * head]
            own_score = lax.dot_general(
                query, kv_all[:block, :head], nt, preferred_element_type=F32) * head ** (-0.5)
            before_score = lax.dot_general(
                query, kv_all[block:, :head], nt, preferred_element_type=F32) * head ** (-0.5)
            own_score = jnp.where(own_visible, own_score, -1e30)
            before_score = jnp.where(before_visible, before_score, -1e30)
            top = jnp.maximum(
                jnp.max(own_score, axis=1, keepdims=True), jnp.max(before_score, axis=1, keepdims=True))
            own_w = jnp.where(own_visible, jnp.exp(own_score - top), 0.0)
            before_w = jnp.where(before_visible, jnp.exp(before_score - top), 0.0)
            total = jnp.sum(own_w, axis=1, keepdims=True) + jnp.sum(before_w, axis=1, keepdims=True)
            mixed = jnp.dot(own_w.astype(BF16), kv_all[:block, head:], preferred_element_type=F32)
            mixed += jnp.dot(before_w.astype(BF16), kv_all[block:, head:], preferred_element_type=F32)
            parts.append((mixed / total).astype(BF16))
        att_own[...] = jnp.concatenate(parts, axis=1)
        for link in range(3):
            send_link(link, lambda link=link: first_attended(link).start())

        def normed_of(resid, attended):
            after_attn = (
                resid.astype(F32) + jnp.dot(attended, proj_ref[...], preferred_element_type=F32)
            ).astype(BF16)
            wide = after_attn.astype(F32)
            normed = wide * lax.rsqrt(jnp.mean(wide * wide, axis=1, keepdims=True) + EPS) * gain_ref[...]
            return after_attn, normed.astype(BF16)

        after_attn, normed = normed_of(resid_ref[...], att_own[...])
        after[...] = after_attn
        tok_rows(z, x)[...] = normed
        for link in range(3):
            send_link(link, lambda link=link: first_normed(link).start())

    def tok_z(way, h):
        step = 1 - 2 * way
        here = tok_rows(z - step * h, x)
        return remote(here, here, z_snd.at[way, h], z_rcv.at[way, h], z_device(z + step))

    def tok_z_arrived(way, h):
        here = tok_rows(z - (1 - 2 * way) * (h + 1), x)
        remote(here, here, z_snd.at[way, h], z_rcv.at[way, h], x_peer).wait_recv()

    def tok_x(zz, xx, part):
        here = tok_rows(zz, xx, part * keep, rows - keep if part else keep)
        return remote(here, here, x_snd.at[part, zz], x_rcv.at[part, zz], x_peer)

    def send_x(zz):
        tok_x(zz, x, 0).start()

        @pl.when(middle(zz))
        def _():
            tok_x(zz, x, 1).start()

    def tok_half(way, to):
        here = tok_rows(last_z if way else 0, 1 - x, keep, rows - keep)
        return remote(here, here, g_snd.at[way], g_rcv.at[way], to)

    def from_origin(way):
        return last_z - z if way else z

    def absorb(link):
        zz, xx = sources[link]

        def act():
            if True:
                first_resid(link).wait_recv()
            if True:
                first_attended(link).wait_recv()
            tok_rows(zz, xx, 0, early)[...] = normed_of(res_in[link], att_in[link])[1]
            if True:
                first_normed(link, (zz, xx)).wait_recv()
            if link == 2:
                for way in range(2):
                    @pl.when(from_origin(way) == 0)
                    def _():
                        tok_half(way, z_device(z + 1 - 2 * way)).start()
            else:
                @pl.when(inside(z + 1 - 2 * link))
                def _():
                    tok_z(link, 1).start()

                send_x(zz)

        if link == 2:
            act()
        else:
            pl.when(inside(zz))(act)

    def pair_of(j):
        return z + ((j + 1) // 2) * (1 - 2 * (j % 2))

    def both_rows(zz):
        return pl.ds(pl.multiple_of(zz * 2 * rows, 2 * rows), 2 * rows)

    def make_gate(zz):
        here = both_rows(zz)
        gates[here, :] = jnp.dot(tok[here, :], wg[...], preferred_element_type=F32)

    def other_x_arrived(zz):
        if True:
            tok_x(zz, 1 - x, 0).wait_recv()

            @pl.when(middle(zz))
            def _():
                tok_x(zz, 1 - x, 1).wait_recv()

    def gate_step(j, carry):
        zz = pair_of(j)

        @pl.when(inside(zz))
        def _():
            @pl.when(j > 0)
            def _():
                other_x_arrived(zz)

            make_gate(zz)

        return carry

    relays = [(k, s) for k in range(2) for s in range(pieces_w)]

    def relay_to(n):
        while relays and n > 0:
            k, s = relays.pop(0)
            relay_weight(k, s)
            n -= 1

    def halves(h):
        for way in range(2):
            @pl.when(from_origin(way) == h + 1)
            def _():
                if True:
                    tok_half(way, x_peer).wait_recv()

                @pl.when(inside(z + 1 - 2 * way))
                def _():
                    tok_half(way, z_device(z + 1 - 2 * way)).start()

    if True:
        for link in range(3):
            absorb(link)
        halves(0)
        relay_to((pieces_w + 1) // 2)
    for h in range(1, nz - 1):
        if True:
            for way in range(2):
                step = 1 - 2 * way
                source = z - step * (h + 1)

                @pl.when(inside(source))
                def _():
                    if True:
                        tok_z_arrived(way, h)
                    if h < nz - 2:
                        @pl.when(inside(z + step))
                        def _():
                            tok_z(way, h + 1).start()

                    send_x(source)
        if h == 1:
            if True:
                relay_to(pieces_w - (pieces_w + 1) // 2)
                weight_ready(0)
            if True:
                lax.fori_loop(0, 3, gate_step, 0)
                relay_to(1)
        else:
            if True:
                relay_to(1)
                lax.fori_loop(2 * h - 1, 2 * h + 1, gate_step, 0)
        if True:
            halves(h)
    if True:
        relay_to(len(relays))
        weight_ready(1)

    def columns_of(chip):
        return lax.rem(i // 2 + chips - chip, chips)

    def end_way(zz):
        return jnp.where(zz == last_z, 0, 1)

    def sum_x(p, zz, part):
        there = pl.ds(part * keep, rows - keep if part else keep)
        return remote(x_out.at[p, zz, there], x_in.at[p, zz, there], rx_snd.at[part, p, zz],
                      rx_rcv.at[part, p, zz], x_peer)

    def sum_z(p, way, zz):
        step = jnp.where(inside(z + 1 - 2 * way), 1 - 2 * way, 0)
        return remote(z_out.at[p, zz], z_in.at[p, way, zz], rz_snd.at[p, zz], rz_rcv.at[p, way, zz],
                      z_device(z + step))

    def sum_half(p, way, to):
        return remote(h_out.at[p, way], h_in.at[p, way], rh_snd.at[p, way], rh_rcv.at[p, way], to)

    def next_z(way):
        return z_device(jnp.clip(z + 1 - 2 * way, 0, last_z))

    def down(chip, cs, zz):
        def half(xx):
            return hidden[pl.ds(pl.multiple_of((zz * 2 + xx) * rows, rows), rows), :]

        both = jnp.concatenate([half(1 - x), half(x)], axis=0)
        for c in cs:
            p = chip * cuts + c
            for q in range(2):
                part = jnp.dot(both, wd[2 * columns_of(chip) + q, c], preferred_element_type=F32)
                here = slice(q * cw, (q + 1) * cw)
                x_out[p, zz, :, here] = part[:rows].astype(BF16)
                own_part[p, zz, :, here] = part[rows:]
                h_own[p, jnp.where(middle(zz), 2, end_way(zz)), :, here] = part[keep:rows]

    def send_sums(p, zz):
        sum_x(p, zz, 0).start()

        @pl.when(middle(zz))
        def _():
            sum_x(p, zz, 1).start()

        for way in range(2):
            @pl.when(jnp.logical_and(from_origin(way) == 0, zz == (0 if way else last_z)))
            def _():
                h_out[p, way] = h_own[p, way].astype(BF16)
                sum_half(p, way, next_z(way)).start()

    turns = 2 * nz - 1

    def owner(j):
        way = j % 2
        return way, z + (nz - 1 - j // 2) * (1 - 2 * way)

    def finish_half(p, way):
        sum_half(p, way, x_peer).wait_recv()
        h_out[p, way] = (h_own[p, way] + h_in[p, way].astype(F32)).astype(BF16)
        sum_half(p, way, next_z(way)).start()

    near_way = jnp.where(2 * z < nz, 0, 1)

    def relay_half(p, way):
        @pl.when(middle(z))
        def _():
            if True:
                finish_half(p, way)

    def own_half(p):
        for way in range(2):
            @pl.when(z == (0 if way else last_z))
            def _():
                sum_half(p, way, x_peer).wait_recv()
                x_out[p, z, keep:, :] = (h_own[p, way] + h_in[p, way].astype(F32)).astype(BF16)
                sum_x(p, z, 1).start()

    def finish(p, way, zz):
        more = inside(z - (1 - 2 * way))

        @pl.when(inside(zz))
        def _():
            if True:
                sum_x(p, zz, 0).wait_recv()

                @pl.when(middle(zz))
                def _():
                    sum_x(p, zz, 1).wait_recv()

            @pl.when(more)
            def _():
                if True:
                    sum_z(p, way, zz).wait_recv()
                z_out[p, zz] = (
                    own_part[p, zz] + x_in[p, zz].astype(F32) + z_in[p, way, zz].astype(F32)
                ).astype(BF16)

            @pl.when(jnp.logical_not(more))
            def _():
                z_out[p, zz] = (own_part[p, zz] + x_in[p, zz].astype(F32)).astype(BF16)

            sum_z(p, way, zz).start()

    def wd_local(s):
        w_local(2, s).wait()
        w_arrived(2, partner, s)

    for s in range(cuts):
        wd_local(s)

    lag = 4

    def hidden_step(j, carry):
        _, zz = owner(j)

        @pl.when(inside(zz))
        def _():
            @pl.when(jnp.logical_or(j < 2, nz < 3))
            def _():
                @pl.when(j < turns - 1)
                def _():
                    other_x_arrived(zz)

                make_gate(zz)

            here = both_rows(zz)
            gate = gates[here, :]
            upward = jnp.dot(tok[here, :], wu[...], preferred_element_type=F32)
            hidden[here, :] = (gate / (1.0 + jnp.exp(-gate)) * upward).astype(BF16)
            down(0, range(cuts), zz)

            @pl.when(j < turns - 1)
            def _():
                send_sums(0, zz)

        @pl.when(jnp.logical_and(j >= lag, jnp.logical_not(middle(z))))
        def _():
            finish(0, *owner(j - lag))

        return carry

    if True:
        lax.fori_loop(0, turns, hidden_step, 0)

    def send_step(t, carry):
        p = t // (turns - 1)
        _, zz = owner(t % (turns - 1))

        @pl.when(inside(zz))
        def _():
            send_sums(p, zz)

        return carry

    lax.fori_loop(turns - 1, cuts * (turns - 1), send_step, 0)

    def finish_way(p, way, start=0):
        def step(n, carry):
            finish(p, way, z + (nz - 1 - n) * (1 - 2 * way))
            return carry

        lax.fori_loop(start, nz - 1, step, 0)

    def finishes(p, start=0):
        near = near_way
        if True:
            relay_half(p, near)
            finish_way(p, near, start)
        if True:
            relay_half(p, 1 - near)
            finish_way(p, 1 - near, start)

    def far_down(s):
        if True:
            relay_weight(2, s)
            for d in range(1, chips):
                w_arrived(2, lax.rem(partner + 2 * d, n_in), s)

        def step(t, carry):
            chip = 1 + t // turns
            j = t % turns
            _, zz = owner(j)

            @pl.when(inside(zz))
            def _():
                down(chip, (s,), zz)

                @pl.when(j < turns - 1)
                def _():
                    send_sums(chip * cuts + s, zz)

            return carry

        if True:
            lax.fori_loop(0, (chips - 1) * turns, step, 0)

    @pl.when(middle(z))
    def _():
        finishes(0)

    @pl.when(jnp.logical_not(middle(z)))
    def _():
        def step(j, carry):
            finish(0, *owner(j))
            return carry

        lax.fori_loop(turns - lag, turns - 1, step, 0)

    todo = list(range(cuts)) + [c * cuts + s for s in range(cuts) for c in range(1, chips)]
    for p in range(1, cuts):
        far_down(p - 1)
        if True:
            finishes(p)
    far_down(cuts - 1)
    for p in range(parts_n):
        sum_x(p, z, 0).start()

        @pl.when(middle(z))
        def _():
            sum_x(p, z, 1).start()
    for p in todo[cuts:]:
        if True:
            finishes(p)

    if True:
        for p in range(parts_n):
            own_half(p)
    if True:
        for p in range(parts_n):
            for way in range(2):
                @pl.when(inside(z - (1 - 2 * way)))
                def _():
                    sum_z(p, way, z).wait_recv()
                    own_part[p, z] = own_part[p, z] + z_in[p, way, z].astype(F32)
            for part in range(2):
                sum_x(p, z, part).wait_recv()
            for q in range(2):
                source = 2 * columns_of(p // cuts) + q
                here = pl.ds(pl.multiple_of(source * width + (p % cuts) * cw, cw), cw)
                cols = slice(q * cw, (q + 1) * cw)
                out_ref[:, here] = (
                    after[:, here].astype(F32)
                    + (own_part[p, z, :, cols] + x_in[p, z, :, cols].astype(F32))).astype(BF16)

    for d in steps:
        kv_send(0, d).wait_send()
    for d in range(chips):
        kv_relay(0, d).wait_send()

    @pl.when(o < n_out - 1)
    def _():
        for d in range(chips):
            kv_send(1, d).wait_send()

    @pl.when(o > 0)
    def _():
        for d in range(chips):
            kv_relay(1, d).wait_send()

    for link in range(3):
        def sent(link=link):
            first_resid(link).wait_send()
            first_attended(link).wait_send()
            first_normed(link).wait_send()

        send_link(link, sent)
    for k in range(3):
        for s in range(w_parts(k)):
            w_pair(k, s).wait_send()
            for d in steps:
                w_far(k, d, s).wait_send()
                w_relay(k, d, s).wait_send()
    for way in range(2):
        step = 1 - 2 * way

        @pl.when(inside(z + step))
        def _():
            tok_half(way, x_peer).wait_send()
            for h in range(1, nz - 1):
                @pl.when(inside(z - step * h))
                def _():
                    tok_z(way, h).wait_send()
            for p in range(parts_n):
                sum_half(p, way, x_peer).wait_send()
    for zz in range(nz):
        ends = zz == 0 or zz == last_z

        @pl.when(z != zz)
        def _():
            tok_x(zz, x, 0).wait_send()
            if not ends:
                tok_x(zz, x, 1).wait_send()

        for p in range(parts_n):
            sum_x(p, zz, 0).wait_send()
            if not ends:
                sum_x(p, zz, 1).wait_send()
            else:
                @pl.when(z == zz)
                def _():
                    sum_x(p, zz, 1).wait_send()

            @pl.when(z != zz)
            def _():
                sum_z(p, 0, zz).wait_send()


def per_device(n_out, n_in, resid, queries, keyvals, piece_order, out_proj, mlp_gain, w_gate, w_up, w_down):
    rows, model = resid.shape
    units, width = w_down.shape
    nz, chips = n_out // 2, n_in // 2
    cuts = max(1, width // 256)
    pieces_w = max(1, 16 // n_in)
    cw = width // cuts
    parts_n = chips * cuts
    early = rows * 3 // 4
    dma = pltpu.SemaphoreType.DMA
    vmem = pl.BlockSpec(memory_space=pltpu.VMEM)
    hbm = pl.BlockSpec(memory_space=pl.ANY)
    spl = max(cuts, pieces_w)
    half = rows - rows // 2
    return pl.pallas_call(
        functools.partial(layer_kernel, n_out, n_in, cuts, pieces_w, early),
        out_shape=jax.ShapeDtypeStruct(resid.shape, BF16),
        in_specs=[pl.BlockSpec(memory_space=pltpu.SMEM)] + [vmem] * 5 + [hbm] * 3,
        out_specs=vmem,
        scratch_shapes=[
            pltpu.VMEM((2 * n_in * rows, keyvals.shape[1]), BF16),
            pltpu.VMEM((model, units), BF16),
            pltpu.VMEM((model, units), BF16),
            pltpu.VMEM((n_in, cuts, units, cw), BF16),
            pltpu.VMEM((n_out * rows, model), BF16),
            pltpu.VMEM((rows, model), BF16),
            pltpu.VMEM(queries.shape, BF16),
            pltpu.VMEM((3, early, model), BF16),
            pltpu.VMEM((3, early, queries.shape[1]), BF16),
            pltpu.VMEM((n_out * rows, units), F32),
            pltpu.VMEM((n_out * rows, units), BF16),
            pltpu.VMEM((parts_n, nz, rows, 2 * cw), BF16),
            pltpu.VMEM((parts_n, nz, rows, 2 * cw), BF16),
            pltpu.VMEM((parts_n, nz, rows, 2 * cw), F32),
            pltpu.VMEM((parts_n, nz, rows, 2 * cw), BF16),
            pltpu.VMEM((parts_n, 2, nz, rows, 2 * cw), BF16),
            pltpu.VMEM((parts_n, 3, half, 2 * cw), F32),
            pltpu.VMEM((parts_n, 2, half, 2 * cw), BF16),
            pltpu.VMEM((parts_n, 2, half, 2 * cw), BF16),
            dma(()), dma((2, n_in)), dma((2, n_in)), dma((2, n_in)),
            dma((3, spl)), dma((3, spl)), dma((3, n_in, spl)), dma((3, n_in, spl)), dma((3, n_in, spl)),
            dma((3,)), dma((3,)), dma((3,)), dma((3,)), dma((3,)), dma((3,)),
            dma((2, nz)), dma((2, nz)), dma((2,)), dma((2,)), dma((2, nz)), dma((2, nz)),
            dma((2, parts_n, nz)), dma((2, parts_n, nz)), dma((parts_n, nz)), dma((parts_n, 2, nz)),
            dma((parts_n, 2)), dma((parts_n, 2)),
        ],
        compiler_params=pltpu.CompilerParams(
            collective_id=0, has_side_effects=True, vmem_limit_bytes=63000 * 1024
        ),
        name="layer",
    )(piece_order, resid, queries, keyvals, out_proj, mlp_gain.reshape(1, -1), w_gate, w_up, w_down)


def solution(mesh):
    placed = (
        P(("outer", "inner"), None),
        P(("outer", "inner"), None),
        P(("outer", "inner"), None),
        P(),
        P(),
        P(),
        P("inner", "outer"),
        P("inner", "outer"),
        P("outer", "inner"),
    )
    return jax.shard_map(
        functools.partial(per_device, mesh.shape["outer"], mesh.shape["inner"]),
        mesh=mesh,
        in_specs=placed,
        out_specs=P(("outer", "inner"), None),
        check_vma=False,
    )
```

time: 118 us -> 113 us (0.958)
  Pallas kernels: 116 us -> 111 us
    pallas_call x1, Pallas kernels: 116 us -> 111 us  [per_device(): pl.pallas_call(functools.partial(layer_kernel, n_out, n_in, cuts, pieces_...]
where the time goes in v1:
time: 113 us
  Pallas kernels  111 us (98%)
  local copies, waits for them, and re-layouts  1.88 us (2%)
    pallas_call x1, Pallas kernels, per_device(): pl.pallas_call(functools.partial(layer_kernel, n_out, n_in, cuts, pieces_...  111 us

profile of v1, /device:TPU:0, one launch (start us, length us, event | category | flops | bytes accessed | tf_op | source)
XLA Modules:
  0.0 112.9 jit_solution(5155650555621507421)
XLA Ops:
  0.0 111.0 %layer.1 = bf16[128,2048]{1,0:T(8,128)(2,1)} custom-call(s32[8]{0:T(128)} %order_ref.1, bf16[128,2048]{1,0:T(8,128)(2,1)} %resid_ref.1, bf16[128,256]{1,0:T(8,128)(2,1)} %query_ref.1, bf16[128,256]{1,0:T(8,128)(2,1)} %kv_ref.1, bf16[256,2048]{1,0:T(8,128)(2,1)} %proj_ref.1, f32[1,2048]{1,0:T(1,128)} %bitcast.1, bf16[512,896]{1,0:T(8,128)(2,1)} %wg_ref.1, ...), custom_call_target="tpu_custom_call" | custom-call | tf_op jit(solution)/shard_map/layer/pallas_call | solution.py:738
  111.0 1.9 %copy.11 = bf16[128,2048]{1,0:T(8,128)(2,1)} copy(bf16[128,2048]{1,0:T(8,128)(2,1)} %layer.1) | data formatting | bytes 1048576

commit v2 on v1

--- a/solution.py
+++ b/solution.py
@@ -15,8 +15,9 @@
 
 def layer_kernel(
     n_out, n_in, cuts, pieces_w, early,
-    order_ref, resid_ref, query_ref, kv_ref, proj_ref, gain_ref, wg_ref, wu_ref, wd_ref,
+    order_ref, resid_hbm, query_hbm, kv_ref, proj_hbm, gain_hbm, wg_ref, wu_ref, wd_ref,
     out_ref,
+    resid_ref, query_ref, proj_ref, gain_ref, in_sem,
     kv_all, wg, wu, wd, tok, after, att_own, res_in, att_in, gates, hidden,
     x_out, x_in, own_part, z_out, z_in, h_own, h_out, h_in,
     kv_loc, kv_snd, kv_relay_snd, kv_rcv, w_loc, w_pair_snd, w_snd, w_relay_snd, w_rcv,
@@ -31,7 +32,7 @@
     partner = i + 1 - 2 * core
     x_peer = (z * 2 + 1 - x, i)
     core_peer = (o, partner)
-    rows = resid_ref.shape[0]
+    rows = resid_hbm.shape[0]
     head = kv_ref.shape[1] // 2
     heads = query_ref.shape[1] // head
     pieces = order_ref.shape[0]
@@ -62,22 +63,33 @@
 
     barrier = pltpu.get_barrier_semaphore()
     after_o, before_o = lax.rem(o + 1, n_out), lax.rem(o + n_out - 1, n_out)
-    count = 0
+
+    def greet(device):
+        pl.semaphore_signal(barrier, inc=1, device_id=device, device_id_type=MESH)
+
     for d in range(1, n_in):
-        pl.semaphore_signal(barrier, inc=1, device_id=(o, lax.rem(i + d, n_in)), device_id_type=MESH)
-        count += 1
-    for d in range(n_in // 2):
-        for there in (after_o, before_o):
-            pl.semaphore_signal(
-                barrier, inc=1, device_id=(there, lax.rem(i + 2 * d, n_in)), device_id_type=MESH)
-            count += 1
-    for d in range(1, nz):
-        pl.semaphore_signal(
-            barrier, inc=1, device_id=(lax.rem(z + d, nz) * 2 + x, i), device_id_type=MESH)
-        count += 1
-    pl.semaphore_signal(barrier, inc=1, device_id=x_peer, device_id_type=MESH)
-    count += 1
-    pl.semaphore_wait(barrier, count)
+        greet((o, lax.rem(i + d, n_in)))
+    greet(x_peer)
+    pl.when(z > 0)(lambda: greet(z_device(z - 1)))
+    pl.when(z < last_z)(lambda: greet(z_device(z + 1)))
+
+    @pl.when(o > 0)
+    def _():
+        for d in range(chips):
+            greet((before_o, lax.rem(i + 2 * d, n_in)))
+
+    loads = [
+        pltpu.make_async_copy(src, dst, in_sem.at[n])
+        for n, (src, dst) in enumerate((
+            (query_hbm, query_ref), (resid_hbm, resid_ref), (proj_hbm, proj_ref), (gain_hbm, gain_ref)))
+    ]
+    for load in loads:
+        load.start()
+
+    if True:
+        pl.semaphore_wait(
+            barrier, n_in + jnp.where(z > 0, 1, 0) + jnp.where(z < last_z, 1, 0)
+            + jnp.where(o < n_out - 1, chips, 0))
 
     own_rows = pl.ds(pl.multiple_of(i * rows, rows), rows)
     kv_copy = pltpu.make_async_copy(kv_ref, kv_all.at[own_rows], kv_loc)
@@ -114,20 +126,22 @@
     def tok_rows(zz, xx, start=0, size=rows):
         return tok.at[pl.ds(pl.multiple_of((zz * 2 + xx) * rows + start, 16), size)]
 
-    targets = (z_device(z + 1), z_device(z - 1), x_peer)
-    sources = ((z - 1, x), (z + 1, x), (z, 1 - x))
+    def target(link):
+        if isinstance(link, int):
+            return x_peer if link == 2 else z_device(z + 1 - 2 * link)
+        return z_device(z + 1 - 2 * link)
 
     def first_resid(link):
-        return remote(resid_ref.at[pl.ds(0, early)], res_in.at[link], r_snd.at[link], r_rcv.at[link],
-                      targets[link])
+        return remote(resid_hbm.at[pl.ds(0, early)], res_in.at[link], r_snd.at[link], r_rcv.at[link],
+                      target(link))
 
     def first_attended(link):
         return remote(att_own.at[pl.ds(0, early)], att_in.at[link], a_snd.at[link], a_rcv.at[link],
-                      targets[link])
+                      target(link))
 
     def first_normed(link, source=None):
         here = tok_rows(*(source or (z, x)), early, rows - early)
-        return remote(here, here, n_snd.at[link], n_rcv.at[link], targets[link])
+        return remote(here, here, n_snd.at[link], n_rcv.at[link], target(link))
 
     def send_link(link, act):
         if link == 2:
@@ -236,6 +250,7 @@
             kv_arrived(1, lax.rem(partner + 2 * d, n_in))
 
     if True:
+        loads[0].wait()
         parts = []
         nt = (((1,), (1,)), ((), ()))
         for h in range(heads):
@@ -258,6 +273,9 @@
         for link in range(3):
             send_link(link, lambda link=link: first_attended(link).start())
 
+        for load in loads[1:]:
+            load.wait()
+
         def normed_of(resid, attended):
             after_attn = (
                 resid.astype(F32) + jnp.dot(attended, proj_ref[...], preferred_element_type=F32)
@@ -272,25 +290,35 @@
         for link in range(3):
             send_link(link, lambda link=link: first_normed(link).start())
 
-    def tok_z(way, h):
+    def part_rows(zz, xx, part):
+        return tok_rows(zz, xx, part * early, rows - early if part else early)
+
+    def tok_z(way, h, part):
         step = 1 - 2 * way
-        here = tok_rows(z - step * h, x)
-        return remote(here, here, z_snd.at[way, h], z_rcv.at[way, h], z_device(z + step))
-
-    def tok_z_arrived(way, h):
-        here = tok_rows(z - (1 - 2 * way) * (h + 1), x)
-        remote(here, here, z_snd.at[way, h], z_rcv.at[way, h], x_peer).wait_recv()
+        here = part_rows(z - step * h, x, part)
+        return remote(here, here, z_snd.at[part, way, h], z_rcv.at[part, way, h], z_device(z + step))
+
+    def tok_z_arrived(way, h, part):
+        here = part_rows(z - (1 - 2 * way) * (h + 1), x, part)
+        remote(here, here, z_snd.at[part, way, h], z_rcv.at[part, way, h], x_peer).wait_recv()
 
     def tok_x(zz, xx, part):
-        here = tok_rows(zz, xx, part * keep, rows - keep if part else keep)
+        here = part_rows(zz, xx, part)
         return remote(here, here, x_snd.at[part, zz], x_rcv.at[part, zz], x_peer)
 
-    def send_x(zz):
-        tok_x(zz, x, 0).start()
-
+    def tok_x_end(zz, xx):
+        here = tok_rows(zz, xx, 0, keep)
+        return remote(here, here, x_snd.at[0, zz], x_rcv.at[0, zz], x_peer)
+
+    def send_x(zz, part):
         @pl.when(middle(zz))
         def _():
-            tok_x(zz, x, 1).start()
+            tok_x(zz, x, part).start()
+
+        if part == 0:
+            @pl.when(jnp.logical_not(middle(zz)))
+            def _():
+                tok_x_end(zz, x).start()
 
     def tok_half(way, to):
         here = tok_rows(last_z if way else 0, 1 - x, keep, rows - keep)
@@ -299,33 +327,32 @@
     def from_origin(way):
         return last_z - z if way else z
 
-    def absorb(link):
-        zz, xx = sources[link]
-
-        def act():
+    near_way = jnp.where(2 * z < nz, 0, 1)
+
+    def absorb(link, zz, xx):
+        first_resid(link).wait_recv()
+        first_attended(link).wait_recv()
+        tok_rows(zz, xx, 0, early)[...] = normed_of(res_in[link], att_in[link])[1]
+
+    def hop(h, part, way):
+        step = 1 - 2 * way
+        source = z - step * (h + 1)
+
+        @pl.when(inside(source))
+        def _():
             if True:
-                first_resid(link).wait_recv()
-            if True:
-                first_attended(link).wait_recv()
-            tok_rows(zz, xx, 0, early)[...] = normed_of(res_in[link], att_in[link])[1]
-            if True:
-                first_normed(link, (zz, xx)).wait_recv()
-            if link == 2:
-                for way in range(2):
-                    @pl.when(from_origin(way) == 0)
+                if h > 0:
+                    tok_z_arrived(way, h, part)
+                elif part == 0:
+                    absorb(way, source, x)
+                else:
+                    first_normed(way, (source, x)).wait_recv()
+                if h < nz - 2:
+                    @pl.when(inside(z + step))
                     def _():
-                        tok_half(way, z_device(z + 1 - 2 * way)).start()
-            else:
-                @pl.when(inside(z + 1 - 2 * link))
-                def _():
-                    tok_z(link, 1).start()
-
-                send_x(zz)
-
-        if link == 2:
-            act()
-        else:
-            pl.when(inside(zz))(act)
+                        tok_z(way, h + 1, part).start()
+
+                send_x(source, part)
 
     def pair_of(j):
         return z + ((j + 1) // 2) * (1 - 2 * (j % 2))
@@ -339,11 +366,14 @@
 
     def other_x_arrived(zz):
         if True:
-            tok_x(zz, 1 - x, 0).wait_recv()
-
             @pl.when(middle(zz))
             def _():
+                tok_x(zz, 1 - x, 0).wait_recv()
                 tok_x(zz, 1 - x, 1).wait_recv()
+
+            @pl.when(jnp.logical_not(middle(zz)))
+            def _():
+                tok_x_end(zz, 1 - x).wait_recv()
 
     def gate_step(j, carry):
         zz = pair_of(j)
@@ -377,40 +407,31 @@
                 def _():
                     tok_half(way, z_device(z + 1 - 2 * way)).start()
 
-    if True:
-        for link in range(3):
-            absorb(link)
-        halves(0)
-        relay_to((pieces_w + 1) // 2)
-    for h in range(1, nz - 1):
-        if True:
-            for way in range(2):
-                step = 1 - 2 * way
-                source = z - step * (h + 1)
-
-                @pl.when(inside(source))
-                def _():
-                    if True:
-                        tok_z_arrived(way, h)
-                    if h < nz - 2:
-                        @pl.when(inside(z + step))
-                        def _():
-                            tok_z(way, h + 1).start()
-
-                    send_x(source)
-        if h == 1:
+    for h in range(nz - 1):
+        for part in range(2):
+            hop(h, part, 1 - near_way)
+            hop(h, part, near_way)
+        if h == 0:
+            if True:
+                absorb(2, z, 1 - x)
+                first_normed(2, (z, 1 - x)).wait_recv()
+                for way in range(2):
+                    @pl.when(from_origin(way) == 0)
+                    def _():
+                        tok_half(way, z_device(z + 1 - 2 * way)).start()
+            relay_to((pieces_w + 1) // 2)
+        elif h == 1:
             if True:
                 relay_to(pieces_w - (pieces_w + 1) // 2)
                 weight_ready(0)
             if True:
                 lax.fori_loop(0, 3, gate_step, 0)
-                relay_to(1)
+            relay_to(1)
         else:
+            relay_to(1)
             if True:
-                relay_to(1)
                 lax.fori_loop(2 * h - 1, 2 * h + 1, gate_step, 0)
-        if True:
-            halves(h)
+        halves(h)
     if True:
         relay_to(len(relays))
         weight_ready(1)
@@ -458,11 +479,13 @@
         def _():
             sum_x(p, zz, 1).start()
 
+    def send_halves(ps, zz):
         for way in range(2):
             @pl.when(jnp.logical_and(from_origin(way) == 0, zz == (0 if way else last_z)))
             def _():
-                h_out[p, way] = h_own[p, way].astype(BF16)
-                sum_half(p, way, next_z(way)).start()
+                for p in ps:
+                    h_out[p, way] = h_own[p, way].astype(BF16)
+                    sum_half(p, way, next_z(way)).start()
 
     turns = 2 * nz - 1
 
@@ -474,8 +497,6 @@
         sum_half(p, way, x_peer).wait_recv()
         h_out[p, way] = (h_own[p, way] + h_in[p, way].astype(F32)).astype(BF16)
         sum_half(p, way, next_z(way)).start()
-
-    near_way = jnp.where(2 * z < nz, 0, 1)
 
     def relay_half(p, way):
         @pl.when(middle(z))
@@ -529,6 +550,11 @@
     def hidden_step(j, carry):
         _, zz = owner(j)
 
+        @pl.when(jnp.logical_and(j >= lag, jnp.logical_not(middle(z))))
+        def _():
+            for p in range(cuts):
+                finish(p, *owner(j - lag))
+
         @pl.when(inside(zz))
         def _():
             @pl.when(jnp.logical_or(j < 2, nz < 3))
@@ -547,44 +573,51 @@
 
             @pl.when(j < turns - 1)
             def _():
-                send_sums(0, zz)
-
-        @pl.when(jnp.logical_and(j >= lag, jnp.logical_not(middle(z))))
-        def _():
-            finish(0, *owner(j - lag))
+                for p in range(cuts):
+                    send_sums(p, zz)
+                send_halves(range(cuts), zz)
 
         return carry
 
     if True:
         lax.fori_loop(0, turns, hidden_step, 0)
 
-    def send_step(t, carry):
-        p = t // (turns - 1)
-        _, zz = owner(t % (turns - 1))
-
-        @pl.when(inside(zz))
-        def _():
-            send_sums(p, zz)
-
-        return carry
-
-    lax.fori_loop(turns - 1, cuts * (turns - 1), send_step, 0)
-
-    def finish_way(p, way, start=0):
+    near_end = jnp.where(near_way == 0, last_z, 0)
+
+    def finish_end(p):
+        if True:
+            relay_half(p, near_way)
+            finish(p, near_way, near_end)
+
+    def finish_way(p, way, skip):
         def step(n, carry):
-            finish(p, way, z + (nz - 1 - n) * (1 - 2 * way))
+            zz = z + (nz - 1 - n) * (1 - 2 * way)
+
+            @pl.when(zz != skip)
+            def _():
+                finish(p, way, zz)
+
             return carry
 
+        lax.fori_loop(0, nz - 1, step, 0)
+
+    def finish_middle(ps):
+        for p in ps:
+            if True:
+                relay_half(p, 1 - near_way)
+                finish_way(p, 1 - near_way, -1)
+            if True:
+                finish_way(p, near_way, near_end)
+
+    def finish_outer(ps, start, done=0):
+        def step(n, carry):
+            @pl.when(n >= done)
+            def _():
+                for p in ps:
+                    finish(p, near_way, z + (nz - 1 - n) * (1 - 2 * near_way))
+            return carry
+
         lax.fori_loop(start, nz - 1, step, 0)
-
-    def finishes(p, start=0):
-        near = near_way
-        if True:
-            relay_half(p, near)
-            finish_way(p, near, start)
-        if True:
-            relay_half(p, 1 - near)
-            finish_way(p, 1 - near, start)
 
     def far_down(s):
         if True:
@@ -604,6 +637,7 @@
                 @pl.when(j < turns - 1)
                 def _():
                     send_sums(chip * cuts + s, zz)
+                    send_halves((chip * cuts + s,), zz)
 
             return carry
 
@@ -612,37 +646,114 @@
 
     @pl.when(middle(z))
     def _():
-        finishes(0)
+        for p in range(cuts):
+            finish_end(p)
+        finish_middle(range(cuts))
 
     @pl.when(jnp.logical_not(middle(z)))
     def _():
-        def step(j, carry):
-            finish(0, *owner(j))
-            return carry
-
-        lax.fori_loop(turns - lag, turns - 1, step, 0)
-
-    todo = list(range(cuts)) + [c * cuts + s for s in range(cuts) for c in range(1, chips)]
-    for p in range(1, cuts):
-        far_down(p - 1)
-        if True:
-            finishes(p)
-    far_down(cuts - 1)
-    for p in range(parts_n):
-        sum_x(p, z, 0).start()
-
-        @pl.when(middle(z))
-        def _():
-            sum_x(p, z, 1).start()
-    for p in todo[cuts:]:
-        if True:
-            finishes(p)
+        finish_outer(range(cuts), (turns - lag) // 2, jnp.where(near_way == 0, (turns - lag + 1) // 2, 0))
+
+    rest = [c * cuts + s for s in range(cuts) for c in range(1, chips)]
+
+    def drain_first():
+        for d in steps:
+            kv_send(0, d).wait_send()
+        for d in range(chips):
+            kv_relay(0, d).wait_send()
+
+        @pl.when(o < n_out - 1)
+        def _():
+            for d in range(chips):
+                kv_send(1, d).wait_send()
+
+        @pl.when(o > 0)
+        def _():
+            for d in range(chips):
+                kv_relay(1, d).wait_send()
+
+        for link in range(3):
+            def sent(link=link):
+                first_resid(link).wait_send()
+                first_attended(link).wait_send()
+                first_normed(link).wait_send()
+
+            send_link(link, sent)
+        for way in range(2):
+            step = 1 - 2 * way
+
+            @pl.when(inside(z + step))
+            def _():
+                tok_half(way, x_peer).wait_send()
+                for h in range(1, nz - 1):
+                    @pl.when(inside(z - step * h))
+                    def _():
+                        tok_z(way, h, 0).wait_send()
+                        tok_z(way, h, 1).wait_send()
+        for zz in range(nz):
+            @pl.when(z != zz)
+            def _():
+                if zz == 0 or zz == last_z:
+                    tok_x_end(zz, x).wait_send()
+                else:
+                    tok_x(zz, x, 0).wait_send()
+                    tok_x(zz, x, 1).wait_send()
+
+    def drain_weights(k):
+        for s in range(w_parts(k)):
+            w_pair(k, s).wait_send()
+            for d in steps:
+                w_far(k, d, s).wait_send()
+                w_relay(k, d, s).wait_send()
+
+    def drain_sums(p):
+        for way in range(2):
+            @pl.when(inside(z + 1 - 2 * way))
+            def _():
+                sum_half(p, way, x_peer).wait_send()
+        for zz in range(nz):
+            sum_x(p, zz, 0).wait_send()
+            if 0 < zz < last_z:
+                sum_x(p, zz, 1).wait_send()
+            else:
+                @pl.when(z == zz)
+                def _():
+                    sum_x(p, zz, 1).wait_send()
+
+            @pl.when(z != zz)
+            def _():
+                sum_z(p, 0, zz).wait_send()
+
+    if True:
+        drain_first()
+    for s in range(cuts):
+        far_down(s)
+        if s == cuts - 1:
+            for p in range(parts_n):
+                sum_x(p, z, 0).start()
+
+                @pl.when(middle(z))
+                def _():
+                    sum_x(p, z, 1).start()
+        for c in range(1, chips):
+            finish_end(c * cuts + s)
+    if True:
+        for k in range(3):
+            drain_weights(k)
+
+    @pl.when(middle(z))
+    def _():
+        finish_middle(rest)
+
+    @pl.when(jnp.logical_not(middle(z)))
+    def _():
+        finish_outer(rest, 1)
 
     if True:
         for p in range(parts_n):
             own_half(p)
-    if True:
-        for p in range(parts_n):
+    for p in range(parts_n):
+        if True:
             for way in range(2):
                 @pl.when(inside(z - (1 - 2 * way)))
                 def _():
@@ -657,68 +768,10 @@
                 out_ref[:, here] = (
                     after[:, here].astype(F32)
                     + (own_part[p, z, :, cols] + x_in[p, z, :, cols].astype(F32))).astype(BF16)
-
-    for d in steps:
-        kv_send(0, d).wait_send()
-    for d in range(chips):
-        kv_relay(0, d).wait_send()
-
-    @pl.when(o < n_out - 1)
-    def _():
-        for d in range(chips):
-            kv_send(1, d).wait_send()
-
-    @pl.when(o > 0)
-    def _():
-        for d in range(chips):
-            kv_relay(1, d).wait_send()
-
-    for link in range(3):
-        def sent(link=link):
-            first_resid(link).wait_send()
-            first_attended(link).wait_send()
-            first_normed(link).wait_send()
-
-        send_link(link, sent)
-    for k in range(3):
-        for s in range(w_parts(k)):
-            w_pair(k, s).wait_send()
-            for d in steps:
-                w_far(k, d, s).wait_send()
-                w_relay(k, d, s).wait_send()
-    for way in range(2):
-        step = 1 - 2 * way
-
-        @pl.when(inside(z + step))
-        def _():
-            tok_half(way, x_peer).wait_send()
-            for h in range(1, nz - 1):
-                @pl.when(inside(z - step * h))
-                def _():
-                    tok_z(way, h).wait_send()
-            for p in range(parts_n):
-                sum_half(p, way, x_peer).wait_send()
-    for zz in range(nz):
-        ends = zz == 0 or zz == last_z
-
-        @pl.when(z != zz)
-        def _():
-            tok_x(zz, x, 0).wait_send()
-            if not ends:
-                tok_x(zz, x, 1).wait_send()
-
-        for p in range(parts_n):
-            sum_x(p, zz, 0).wait_send()
-            if not ends:
-                sum_x(p, zz, 1).wait_send()
-            else:
-                @pl.when(z == zz)
-                def _():
-                    sum_x(p, zz, 1).wait_send()
-
-            @pl.when(z != zz)
-            def _():
-                sum_z(p, 0, zz).wait_send()
+        if p < parts_n - 1:
+            drain_sums(p)
+
+    drain_sums(parts_n - 1)
 
 
 def per_device(n_out, n_in, resid, queries, keyvals, piece_order, out_proj, mlp_gain, w_gate, w_up, w_down):
@@ -737,10 +790,15 @@
     half = rows - rows // 2
     return pl.pallas_call(
         functools.partial(layer_kernel, n_out, n_in, cuts, pieces_w, early),
-        out_shape=jax.ShapeDtypeStruct(resid.shape, BF16),
-        in_specs=[pl.BlockSpec(memory_space=pltpu.SMEM)] + [vmem] * 5 + [hbm] * 3,
+        out_shape=pltpu.VMEM(resid.shape, BF16),
+        in_specs=[pl.BlockSpec(memory_space=pltpu.SMEM)] + [hbm] * 8,
         out_specs=vmem,
         scratch_shapes=[
+            pltpu.VMEM(resid.shape, BF16),
+            pltpu.VMEM(queries.shape, BF16),
+            pltpu.VMEM(out_proj.shape, BF16),
+            pltpu.VMEM((1, model), F32),
+            dma((4,)),
             pltpu.VMEM((2 * n_in * rows, keyvals.shape[1]), BF16),
             pltpu.VMEM((model, units), BF16),
             pltpu.VMEM((model, units), BF16),
@@ -760,10 +818,10 @@
             pltpu.VMEM((parts_n, 3, half, 2 * cw), F32),
             pltpu.VMEM((parts_n, 2, half, 2 * cw), BF16),
             pltpu.VMEM((parts_n, 2, half, 2 * cw), BF16),
-            dma(()), dma((2, n_in)), dma((2, n_in)), dma((2, n_in)),
-            dma((3, spl)), dma((3, spl)), dma((3, n_in, spl)), dma((3, n_in, spl)), dma((3, n_in, spl)),
+            dma(()), dma((2, chips)), dma((2, chips)), dma((2, n_in)),
+            dma((3, spl)), dma((3, spl)), dma((3, chips, spl)), dma((3, chips, spl)), dma((3, n_in, spl)),
             dma((3,)), dma((3,)), dma((3,)), dma((3,)), dma((3,)), dma((3,)),
-            dma((2, nz)), dma((2, nz)), dma((2,)), dma((2,)), dma((2, nz)), dma((2, nz)),
+            dma((2, 2, nz)), dma((2, 2, nz)), dma((2,)), dma((2,)), dma((2, nz)), dma((2, nz)),
             dma((2, parts_n, nz)), dma((2, parts_n, nz)), dma((parts_n, nz)), dma((parts_n, 2, nz)),
             dma((parts_n, 2)), dma((parts_n, 2)),
         ],

time: 113 us -> 104 us (0.920); the launches traced: 113 us -> 102 us
  Pallas kernels: 111 us -> 101 us
    pallas_call x1, Pallas kernels: 111 us -> 101 us  [per_device(): pl.pallas_call(functools.partial(layer_kernel, n_out, n_in, cuts, pieces_...]
where the time goes in v2:
time: 104 us; the launch traced here: 102 us
  Pallas kernels  101 us (97%)
    pallas_call x1, Pallas kernels, per_device(): pl.pallas_call(functools.partial(layer_kernel, n_out, n_in, cuts, pieces_...  101 us

profile of v2, /device:TPU:0, one launch (start us, length us, event | category | flops | bytes accessed | tf_op | source)
XLA Modules:
  0.0 101.9 jit_solution(32133148735774790)
XLA Ops:
  0.0 101.1 %layer.1 = bf16[128,2048]{1,0:T(8,128)(2,1)S(1)} custom-call(s32[8]{0:T(128)} %order_ref.1, bf16[128,2048]{1,0:T(8,128)(2,1)} %resid_hbm.1, bf16[128,256]{1,0:T(8,128)(2,1)} %query_hbm.1, bf16[128,256]{1,0:T(8,128)(2,1)} %kv_ref.1, bf16[256,2048]{1,0:T(8,128)(2,1)} %proj_hbm.1, f32[1,2048]{1,0:T(1,128)} %bitcast.1, bf16[512,896]{1,0:T(8,128)(2,1)} %wg_ref.1, ...), custom_call_target="tpu_custom_call" | custom-call | tf_op jit(solution)/shard_map/layer/pallas_call | solution.py:791
  101.1 0.8 copy.11

commit v3 on v2

--- a/solution.py
+++ b/solution.py
@@ -20,8 +20,8 @@
     resid_ref, query_ref, proj_ref, gain_ref, in_sem,
     kv_all, wg, wu, wd, tok, after, att_own, res_in, att_in, gates, hidden,
     x_out, x_in, own_part, z_out, z_in, h_own, h_out, h_in,
-    kv_loc, kv_snd, kv_relay_snd, kv_rcv, w_loc, w_pair_snd, w_snd, w_relay_snd, w_rcv,
-    r_snd, r_rcv, a_snd, a_rcv, n_snd, n_rcv, z_snd, z_rcv, g_snd, g_rcv, x_snd, x_rcv,
+    kv_loc, kv_snd, kv_relay_snd, kv_rcv, w_loc, w_pair_snd, w_pair_rcv, w_snd, w_relay_snd, w_rcv,
+    r_snd, r_rcv, a_snd, a_rcv, n_rcv, z_snd, z_rcv, g_snd, g_rcv, x_snd, x_rcv,
     rx_snd, rx_rcv, rz_snd, rz_rcv, rh_snd, rh_rcv,
 ):
     o = lax.axis_index("outer")
@@ -141,7 +141,7 @@
 
     def first_normed(link, source=None):
         here = tok_rows(*(source or (z, x)), early, rows - early)
-        return remote(here, here, n_snd.at[link], n_rcv.at[link], target(link))
+        return remote(here, here, r_snd.at[link], n_rcv.at[link], target(link))
 
     def send_link(link, act):
         if link == 2:
@@ -170,24 +170,56 @@
     def w_parts(k):
         return cuts if k == 2 else pieces_w
 
+    def shard(k, q):
+        if k == 2:
+            return wd.at[q]
+        full = wg if k == 0 else wu
+        return full.at[pl.ds(pl.multiple_of(q * depth, depth), depth)]
+
+    def far(d):
+        return lax.rem(i + n_in - 2 * d, n_in)
+
     def w_far(k, d, s):
-        return remote(w_src(k, s), slot(k, i, s), w_snd.at[k, d, s], w_rcv.at[k, i, s],
+        return remote(w_src(k, s), slot(k, i, s), w_snd.at[k, d], w_rcv.at[k, d - 1, 0, s],
                       (o, lax.rem(i + 2 * d, n_in)))
 
+    def w_relay(k, d, s):
+        here = slot(k, far(d), s)
+        return remote(here, here, w_relay_snd.at[k, d], w_rcv.at[k, d - 1, 1, s], core_peer)
+
     def w_pair(k, s):
-        return remote(w_src(k, s), slot(k, i, s), w_pair_snd.at[k, s], w_rcv.at[k, i, s], core_peer)
-
-    def w_arrived(k, q, s):
-        here = slot(k, q, s)
-        remote(here, here, w_pair_snd.at[k, s], w_rcv.at[k, q, s], core_peer).wait_recv()
-
-    def w_relay(k, d, s):
-        q = lax.rem(i + n_in - 2 * d, n_in)
-        here = slot(k, q, s)
-        return remote(here, here, w_relay_snd.at[k, d, s], w_rcv.at[k, q, s], core_peer)
+        return remote(w_src(k, s), slot(k, i, s), w_pair_snd.at[k], w_pair_rcv.at[k], core_peer)
 
     def w_local(k, s):
-        return pltpu.make_async_copy(w_src(k, s), slot(k, i, s), w_loc.at[k, s])
+        return pltpu.make_async_copy(w_src(k, s), slot(k, i, s), w_loc.at[k])
+
+    def near_ready(k):
+        mine, other = shard(k, i), shard(k, partner)
+        pltpu.make_async_copy(mine, mine, w_loc.at[k]).wait()
+        remote(other, other, w_pair_snd.at[k], w_pair_rcv.at[k], core_peer).wait_recv()
+
+    def far_ready(k, s):
+        for d in steps:
+            here = slot(k, lax.rem(partner + n_in - 2 * d, n_in), s)
+            remote(here, here, w_relay_snd.at[k, d], w_rcv.at[k, d - 1, 1, s], core_peer).wait_recv()
+
+    def relay_weight(k, s):
+        for d in steps:
+            here = slot(k, far(d), s)
+            remote(here, here, w_relay_snd.at[k, d], w_rcv.at[k, d - 1, 0, s], core_peer).wait_recv()
+            w_relay(k, d, s).start()
+
+    def weight_ready(k):
+        near_ready(k)
+        for s in range(w_parts(k)):
+            far_ready(k, s)
+
+    def drain_weights(k):
+        mine = shard(k, i)
+        remote(mine, mine, w_pair_snd.at[k], w_pair_rcv.at[k], core_peer).wait_send()
+        for d in steps:
+            remote(mine, mine, w_snd.at[k, d], w_pair_rcv.at[k], core_peer).wait_send()
+            remote(mine, mine, w_relay_snd.at[k, d], w_pair_rcv.at[k], core_peer).wait_send()
 
     for k in range(3):
         for s in range(w_parts(k)):
@@ -197,17 +229,6 @@
         for s in range(w_parts(k)):
             w_pair(k, s).start()
             w_local(k, s).start()
-
-    def relay_weight(k, s):
-        for d in steps:
-            w_arrived(k, lax.rem(i + n_in - 2 * d, n_in), s)
-            w_relay(k, d, s).start()
-
-    def weight_ready(k):
-        for s in range(w_parts(k)):
-            w_local(k, s).wait()
-            for d in range(chips):
-                w_arrived(k, lax.rem(partner + 2 * d, n_in), s)
 
     lane = lax.broadcasted_iota(jnp.int32, (rows, block), 1)
     key_pos = jnp.zeros((rows, block), jnp.int32)
@@ -296,19 +317,19 @@
     def tok_z(way, h, part):
         step = 1 - 2 * way
         here = part_rows(z - step * h, x, part)
-        return remote(here, here, z_snd.at[part, way, h], z_rcv.at[part, way, h], z_device(z + step))
+        return remote(here, here, z_snd.at[way, h - 1], z_rcv.at[part, way, h - 1], z_device(z + step))
 
     def tok_z_arrived(way, h, part):
         here = part_rows(z - (1 - 2 * way) * (h + 1), x, part)
-        remote(here, here, z_snd.at[part, way, h], z_rcv.at[part, way, h], x_peer).wait_recv()
+        remote(here, here, z_snd.at[way, h - 1], z_rcv.at[part, way, h - 1], x_peer).wait_recv()
 
     def tok_x(zz, xx, part):
         here = part_rows(zz, xx, part)
-        return remote(here, here, x_snd.at[part, zz], x_rcv.at[part, zz], x_peer)
+        return remote(here, here, x_snd.at[zz], x_rcv.at[zz], x_peer)
 
     def tok_x_end(zz, xx):
         here = tok_rows(zz, xx, 0, keep)
-        return remote(here, here, x_snd.at[0, zz], x_rcv.at[0, zz], x_peer)
+        return remote(here, here, x_snd.at[zz], x_rcv.at[zz], x_peer)
 
     def send_x(zz, part):
         @pl.when(middle(zz))
@@ -368,8 +389,8 @@
         if True:
             @pl.when(middle(zz))
             def _():
-                tok_x(zz, 1 - x, 0).wait_recv()
-                tok_x(zz, 1 - x, 1).wait_recv()
+                whole = tok_rows(zz, 1 - x)
+                remote(whole, whole, x_snd.at[zz], x_rcv.at[zz], x_peer).wait_recv()
 
             @pl.when(jnp.logical_not(middle(zz)))
             def _():
@@ -434,6 +455,13 @@
         halves(h)
     if True:
         relay_to(len(relays))
+
+        @pl.when(jnp.logical_not(middle(z)))
+        def _():
+            zz = last_z - z
+            other_x_arrived(zz)
+            make_gate(zz)
+
         weight_ready(1)
 
     def columns_of(chip):
@@ -444,12 +472,17 @@
 
     def sum_x(p, zz, part):
         there = pl.ds(part * keep, rows - keep if part else keep)
-        return remote(x_out.at[p, zz, there], x_in.at[p, zz, there], rx_snd.at[part, p, zz],
-                      rx_rcv.at[part, p, zz], x_peer)
-
-    def sum_z(p, way, zz):
+        return remote(x_out.at[p, zz, there], x_in.at[p, zz, there], rx_snd.at[part, p],
+                      rx_rcv.at[p, zz], x_peer)
+
+    def sum_x_whole(p, zz):
+        return remote(x_out.at[p, zz], x_in.at[p, zz], rx_snd.at[0, p], rx_rcv.at[p, zz], x_peer)
+
+    def sum_z(p, way, zz, here=False):
         step = jnp.where(inside(z + 1 - 2 * way), 1 - 2 * way, 0)
-        return remote(z_out.at[p, zz], z_in.at[p, way, zz], rz_snd.at[p, zz], rz_rcv.at[p, way, zz],
+        off = 0 if here else step
+        return remote(z_out.at[p, zz], z_in.at[p, way, zz], rz_snd.at[p],
+                      rz_rcv.at[p, jnp.where(jnp.logical_and(way == 1, zz == z + off), nz, zz)],
                       z_device(z + step))
 
     def sum_half(p, way, to):
@@ -518,16 +551,18 @@
         @pl.when(inside(zz))
         def _():
             if True:
-                sum_x(p, zz, 0).wait_recv()
-
                 @pl.when(middle(zz))
                 def _():
-                    sum_x(p, zz, 1).wait_recv()
+                    sum_x_whole(p, zz).wait_recv()
+
+                @pl.when(jnp.logical_not(middle(zz)))
+                def _():
+                    sum_x(p, zz, 0).wait_recv()
 
             @pl.when(more)
             def _():
                 if True:
-                    sum_z(p, way, zz).wait_recv()
+                    sum_z(p, way, zz, True).wait_recv()
                 z_out[p, zz] = (
                     own_part[p, zz] + x_in[p, zz].astype(F32) + z_in[p, way, zz].astype(F32)
                 ).astype(BF16)
@@ -538,14 +573,8 @@
 
             sum_z(p, way, zz).start()
 
-    def wd_local(s):
-        w_local(2, s).wait()
-        w_arrived(2, partner, s)
-
-    for s in range(cuts):
-        wd_local(s)
-
-    lag = 4
+    near_ready(2)
+    lag = turns - 2
 
     def hidden_step(j, carry):
         _, zz = owner(j)
@@ -557,14 +586,6 @@
 
         @pl.when(inside(zz))
         def _():
-            @pl.when(jnp.logical_or(j < 2, nz < 3))
-            def _():
-                @pl.when(j < turns - 1)
-                def _():
-                    other_x_arrived(zz)
-
-                make_gate(zz)
-
             here = both_rows(zz)
             gate = gates[here, :]
             upward = jnp.dot(tok[here, :], wu[...], preferred_element_type=F32)
@@ -609,10 +630,9 @@
             if True:
                 finish_way(p, near_way, near_end)
 
-    def finish_outer(ps, start, done=0):
+    def finish_outer(ps, start):
         def step(n, carry):
-            @pl.when(n >= done)
-            def _():
+            if True:
                 for p in ps:
                     finish(p, near_way, z + (nz - 1 - n) * (1 - 2 * near_way))
             return carry
@@ -621,9 +641,7 @@
 
     def far_down(s):
         if True:
-            relay_weight(2, s)
-            for d in range(1, chips):
-                w_arrived(2, lax.rem(partner + 2 * d, n_in), s)
+            far_ready(2, s)
 
         def step(t, carry):
             chip = 1 + t // turns
@@ -644,15 +662,26 @@
         if True:
             lax.fori_loop(0, (chips - 1) * turns, step, 0)
 
+    def own_sums(ps):
+        for p in ps:
+            sum_x(p, z, 0).start()
+
+            @pl.when(middle(z))
+            def _():
+                sum_x(p, z, 1).start()
+
     @pl.when(middle(z))
     def _():
+        own_sums(range(cuts))
         for p in range(cuts):
             finish_end(p)
-        finish_middle(range(cuts))
+        relay_weight(2, 0)
+        finish_middle((0,))
 
     @pl.when(jnp.logical_not(middle(z)))
     def _():
-        finish_outer(range(cuts), (turns - lag) // 2, jnp.where(near_way == 0, (turns - lag + 1) // 2, 0))
+        relay_weight(2, 0)
+        finish(0, near_way, z + (nz - 2) * (1 - 2 * near_way))
 
     rest = [c * cuts + s for s in range(cuts) for c in range(1, chips)]
 
@@ -674,9 +703,9 @@
 
         for link in range(3):
             def sent(link=link):
-                first_resid(link).wait_send()
                 first_attended(link).wait_send()
-                first_normed(link).wait_send()
+                whole = tok_rows(z, x)
+                remote(whole, whole, r_snd.at[link], r_rcv.at[link], target(link)).wait_send()
 
             send_link(link, sent)
         for way in range(2):
@@ -688,53 +717,59 @@
                 for h in range(1, nz - 1):
                     @pl.when(inside(z - step * h))
                     def _():
-                        tok_z(way, h, 0).wait_send()
-                        tok_z(way, h, 1).wait_send()
+                        whole = tok_rows(z, x)
+                        remote(whole, whole, z_snd.at[way, h - 1], z_rcv.at[0, way, h - 1], x_peer).wait_send()
         for zz in range(nz):
             @pl.when(z != zz)
             def _():
                 if zz == 0 or zz == last_z:
                     tok_x_end(zz, x).wait_send()
                 else:
-                    tok_x(zz, x, 0).wait_send()
-                    tok_x(zz, x, 1).wait_send()
-
-    def drain_weights(k):
-        for s in range(w_parts(k)):
-            w_pair(k, s).wait_send()
-            for d in steps:
-                w_far(k, d, s).wait_send()
-                w_relay(k, d, s).wait_send()
+                    whole = tok_rows(zz, x)
+                    remote(whole, whole, x_snd.at[zz], x_rcv.at[zz], x_peer).wait_send()
 
     def drain_sums(p):
         for way in range(2):
             @pl.when(inside(z + 1 - 2 * way))
             def _():
                 sum_half(p, way, x_peer).wait_send()
-        for zz in range(nz):
-            sum_x(p, zz, 0).wait_send()
-            if 0 < zz < last_z:
-                sum_x(p, zz, 1).wait_send()
-            else:
-                @pl.when(z == zz)
-                def _():
-                    sum_x(p, zz, 1).wait_send()
-
-            @pl.when(z != zz)
-            def _():
-                sum_z(p, 0, zz).wait_send()
+        first = x_out.at[p, :, pl.ds(0, keep)]
+        remote(first, first, rx_snd.at[0, p], rx_rcv.at[p, 0], x_peer).wait_send()
+
+        def second(n):
+            there = x_out.at[p, pl.ds(0, n), pl.ds(keep, rows - keep)]
+            remote(there, there, rx_snd.at[1, p], rx_rcv.at[p, 0], x_peer).wait_send()
+
+        pl.when(middle(z))(lambda: second(nz - 2))
+        pl.when(jnp.logical_not(middle(z)))(lambda: second(nz - 1))
+        others = z_out.at[p, pl.ds(0, nz - 1)]
+        remote(others, others, rz_snd.at[p], rz_rcv.at[p, 0], x_peer).wait_send()
 
     if True:
         drain_first()
     for s in range(cuts):
         far_down(s)
-        if s == cuts - 1:
-            for p in range(parts_n):
-                sum_x(p, z, 0).start()
-
-                @pl.when(middle(z))
-                def _():
-                    sum_x(p, z, 1).start()
+        if s == 0:
+            @pl.when(middle(z))
+            def _():
+                finish_middle(range(1, cuts))
+
+            @pl.when(jnp.logical_not(middle(z)))
+            def _():
+                for p in range(1, cuts):
+                    finish(p, near_way, z + (nz - 2) * (1 - 2 * near_way))
+                finish_outer(range(cuts), 2)
+
+        if s < cuts - 1:
+            relay_weight(2, s + 1)
+        else:
+            @pl.when(middle(z))
+            def _():
+                own_sums(range(cuts, parts_n))
+
+            @pl.when(jnp.logical_not(middle(z)))
+            def _():
+                own_sums(range(parts_n))
         for c in range(1, chips):
             finish_end(c * cuts + s)
     if True:
@@ -757,10 +792,9 @@
             for way in range(2):
                 @pl.when(inside(z - (1 - 2 * way)))
                 def _():
-                    sum_z(p, way, z).wait_recv()
+                    sum_z(p, way, z, True).wait_recv()
                     own_part[p, z] = own_part[p, z] + z_in[p, way, z].astype(F32)
-            for part in range(2):
-                sum_x(p, z, part).wait_recv()
+            sum_x_whole(p, z).wait_recv()
             for q in range(2):
                 source = 2 * columns_of(p // cuts) + q
                 here = pl.ds(pl.multiple_of(source * width + (p % cuts) * cw, cw), cw)
@@ -819,10 +853,11 @@
             pltpu.VMEM((parts_n, 2, half, 2 * cw), BF16),
             pltpu.VMEM((parts_n, 2, half, 2 * cw), BF16),
             dma(()), dma((2, chips)), dma((2, chips)), dma((2, n_in)),
-            dma((3, spl)), dma((3, spl)), dma((3, chips, spl)), dma((3, chips, spl)), dma((3, n_in, spl)),
-            dma((3,)), dma((3,)), dma((3,)), dma((3,)), dma((3,)), dma((3,)),
-            dma((2, 2, nz)), dma((2, 2, nz)), dma((2,)), dma((2,)), dma((2, nz)), dma((2, nz)),
-            dma((2, parts_n, nz)), dma((2, parts_n, nz)), dma((parts_n, nz)), dma((parts_n, 2, nz)),
+            dma((3,)), dma((3,)), dma((3,)), dma((3, chips)), dma((3, chips)),
+            dma((3, max(chips - 1, 1), 2, spl)),
+            dma((3,)), dma((3,)), dma((3,)), dma((3,)), dma((3,)),
+            dma((2, nz - 2)), dma((2, 2, nz - 2)), dma((2,)), dma((2,)), dma((nz,)), dma((nz,)),
+            dma((2, parts_n)), dma((parts_n, nz)), dma((parts_n,)), dma((parts_n, nz + 1)),
             dma((parts_n, 2)), dma((parts_n, 2)),
         ],
         compiler_params=pltpu.CompilerParams(

time: 104 us -> 99.1 us (0.953); the launches traced: 102 us -> 99 us
  Pallas kernels: 101 us -> 98.2 us
    pallas_call x1, Pallas kernels: 101 us -> 98.2 us  [per_device(): pl.pallas_call(functools.partial(layer_kernel, n_out, n_in, cuts, pieces_...]
where the time goes in v3:
time: 99.1 us; the launch traced here: 99 us
  Pallas kernels  98.2 us (99%)
    pallas_call x1, Pallas kernels, per_device(): pl.pallas_call(functools.partial(layer_kernel, n_out, n_in, cuts, pieces_...  98.2 us

profile of v3, /device:TPU:0, one launch (start us, length us, event | category | flops | bytes accessed | tf_op | source)
XLA Modules:
  0.0 99.0 jit_solution(810703229372222535)
XLA Ops:
  0.0 98.2 %layer.1 = bf16[128,2048]{1,0:T(8,128)(2,1)S(1)} custom-call(s32[8]{0:T(128)} %order_ref.1, bf16[128,2048]{1,0:T(8,128)(2,1)} %resid_hbm.1, bf16[128,256]{1,0:T(8,128)(2,1)} %query_hbm.1, bf16[128,256]{1,0:T(8,128)(2,1)} %kv_ref.1, bf16[256,2048]{1,0:T(8,128)(2,1)} %proj_hbm.1, f32[1,2048]{1,0:T(1,128)} %bitcast.1, bf16[512,896]{1,0:T(8,128)(2,1)} %wg_ref.1, ...), custom_call_target="tpu_custom_call" | custom-call | tf_op jit(solution)/shard_map/layer/pallas_call | solution.py:825
  98.2 0.8 copy.11

commit v4 on v3

--- a/solution.py
+++ b/solution.py
@@ -11,14 +11,15 @@
 F32 = jnp.float32
 BF16 = jnp.bfloat16
 EPS = 1e-05
+KEEP = 80
 
 
 def layer_kernel(
-    n_out, n_in, cuts, pieces_w, early,
-    order_ref, resid_hbm, query_hbm, kv_ref, proj_hbm, gain_hbm, wg_ref, wu_ref, wd_ref,
+    n_out, n_in, cuts, pieces_w, early, keep,
+    order_hbm, resid_hbm, query_hbm, kv_ref, proj_hbm, gain_hbm, wg_ref, wu_ref, wd_ref,
     out_ref,
-    resid_ref, query_ref, proj_ref, gain_ref, in_sem,
-    kv_all, wg, wu, wd, tok, after, att_own, res_in, att_in, gates, hidden,
+    order_ref, resid_ref, query_ref, proj_ref, gain_ref, in_sem,
+    kv_all, wg, wu, wd, tok, after, att_own, res_in, att_in, gates, upper, hidden,
     x_out, x_in, own_part, z_out, z_in, h_own, h_out, h_in,
     kv_loc, kv_snd, kv_relay_snd, kv_rcv, w_loc, w_pair_snd, w_pair_rcv, w_snd, w_relay_snd, w_rcv,
     r_snd, r_rcv, a_snd, a_rcv, n_rcv, z_snd, z_rcv, g_snd, g_rcv, x_snd, x_rcv,
@@ -43,7 +44,7 @@
     chips = n_in // 2
     parts_n = chips * cuts
     cw = width // cuts
-    keep = rows // 2
+    keep_t = rows // 2
     last_z = nz - 1
 
     def remote(src, dst, ssem, rsem, device):
@@ -81,15 +82,14 @@
     loads = [
         pltpu.make_async_copy(src, dst, in_sem.at[n])
         for n, (src, dst) in enumerate((
-            (query_hbm, query_ref), (resid_hbm, resid_ref), (proj_hbm, proj_ref), (gain_hbm, gain_ref)))
+            (order_hbm, order_ref), (query_hbm, query_ref), (resid_hbm, resid_ref), (proj_hbm, proj_ref), (gain_hbm, gain_ref)))
     ]
     for load in loads:
         load.start()
 
-    if True:
-        pl.semaphore_wait(
-            barrier, n_in + jnp.where(z > 0, 1, 0) + jnp.where(z < last_z, 1, 0)
-            + jnp.where(o < n_out - 1, chips, 0))
+    pl.semaphore_wait(
+        barrier, n_in + jnp.where(z > 0, 1, 0) + jnp.where(z < last_z, 1, 0)
+        + jnp.where(o < n_out - 1, chips, 0))
 
     own_rows = pl.ds(pl.multiple_of(i * rows, rows), rows)
     kv_copy = pltpu.make_async_copy(kv_ref, kv_all.at[own_rows], kv_loc)
@@ -230,6 +230,7 @@
             w_pair(k, s).start()
             w_local(k, s).start()
 
+    loads[0].wait()
     lane = lax.broadcasted_iota(jnp.int32, (rows, block), 1)
     key_pos = jnp.zeros((rows, block), jnp.int32)
     for p in range(pieces):
@@ -270,46 +271,45 @@
         for d in range(chips):
             kv_arrived(1, lax.rem(partner + 2 * d, n_in))
 
-    if True:
-        loads[0].wait()
-        parts = []
-        nt = (((1,), (1,)), ((), ()))
-        for h in range(heads):
-            query = query_ref[:, h * head:(h + 1) * head]
-            own_score = lax.dot_general(
-                query, kv_all[:block, :head], nt, preferred_element_type=F32) * head ** (-0.5)
-            before_score = lax.dot_general(
-                query, kv_all[block:, :head], nt, preferred_element_type=F32) * head ** (-0.5)
-            own_score = jnp.where(own_visible, own_score, -1e30)
-            before_score = jnp.where(before_visible, before_score, -1e30)
-            top = jnp.maximum(
-                jnp.max(own_score, axis=1, keepdims=True), jnp.max(before_score, axis=1, keepdims=True))
-            own_w = jnp.where(own_visible, jnp.exp(own_score - top), 0.0)
-            before_w = jnp.where(before_visible, jnp.exp(before_score - top), 0.0)
-            total = jnp.sum(own_w, axis=1, keepdims=True) + jnp.sum(before_w, axis=1, keepdims=True)
-            mixed = jnp.dot(own_w.astype(BF16), kv_all[:block, head:], preferred_element_type=F32)
-            mixed += jnp.dot(before_w.astype(BF16), kv_all[block:, head:], preferred_element_type=F32)
-            parts.append((mixed / total).astype(BF16))
-        att_own[...] = jnp.concatenate(parts, axis=1)
-        for link in range(3):
-            send_link(link, lambda link=link: first_attended(link).start())
-
-        for load in loads[1:]:
-            load.wait()
-
-        def normed_of(resid, attended):
-            after_attn = (
-                resid.astype(F32) + jnp.dot(attended, proj_ref[...], preferred_element_type=F32)
-            ).astype(BF16)
-            wide = after_attn.astype(F32)
-            normed = wide * lax.rsqrt(jnp.mean(wide * wide, axis=1, keepdims=True) + EPS) * gain_ref[...]
-            return after_attn, normed.astype(BF16)
-
-        after_attn, normed = normed_of(resid_ref[...], att_own[...])
-        after[...] = after_attn
-        tok_rows(z, x)[...] = normed
-        for link in range(3):
-            send_link(link, lambda link=link: first_normed(link).start())
+    loads[1].wait()
+    parts = []
+    nt = (((1,), (1,)), ((), ()))
+    for h in range(heads):
+        query = query_ref[:, h * head:(h + 1) * head]
+        own_score = lax.dot_general(
+            query, kv_all[:block, :head], nt, preferred_element_type=F32) * head ** (-0.5)
+        before_score = lax.dot_general(
+            query, kv_all[block:, :head], nt, preferred_element_type=F32) * head ** (-0.5)
+        own_score = jnp.where(own_visible, own_score, -1e30)
+        before_score = jnp.where(before_visible, before_score, -1e30)
+        top = jnp.maximum(
+            jnp.max(own_score, axis=1, keepdims=True), jnp.max(before_score, axis=1, keepdims=True))
+        own_w = jnp.where(own_visible, jnp.exp(own_score - top), 0.0)
+        before_w = jnp.where(before_visible, jnp.exp(before_score - top), 0.0)
+        total = jnp.sum(own_w, axis=1, keepdims=True) + jnp.sum(before_w, axis=1, keepdims=True)
+        mixed = jnp.dot(own_w.astype(BF16), kv_all[:block, head:], preferred_element_type=F32)
+        mixed += jnp.dot(before_w.astype(BF16), kv_all[block:, head:], preferred_element_type=F32)
+        parts.append((mixed / total).astype(BF16))
+    att_own[...] = jnp.concatenate(parts, axis=1)
+    for link in range(3):
+        send_link(link, lambda link=link: first_attended(link).start())
+
+    for load in loads[2:]:
+        load.wait()
+
+    def normed_of(resid, attended):
+        after_attn = (
+            resid.astype(F32) + jnp.dot(attended, proj_ref[...], preferred_element_type=F32)
+        ).astype(BF16)
+        wide = after_attn.astype(F32)
+        normed = wide * lax.rsqrt(jnp.mean(wide * wide, axis=1, keepdims=True) + EPS) * gain_ref[...]
+        return after_attn, normed.astype(BF16)
+
+    after_attn, normed = normed_of(resid_ref[...], att_own[...])
+    after[...] = after_attn
+    tok_rows(z, x)[...] = normed
+    for link in range(3):
+        send_link(link, lambda link=link: first_normed(link).start())
 
     def part_rows(zz, xx, part):
         return tok_rows(zz, xx, part * early, rows - early if part else early)
@@ -328,7 +328,7 @@
         return remote(here, here, x_snd.at[zz], x_rcv.at[zz], x_peer)
 
     def tok_x_end(zz, xx):
-        here = tok_rows(zz, xx, 0, keep)
+        here = tok_rows(zz, xx, 0, keep_t)
         return remote(here, here, x_snd.at[zz], x_rcv.at[zz], x_peer)
 
     def send_x(zz, part):
@@ -342,7 +342,7 @@
                 tok_x_end(zz, x).start()
 
     def tok_half(way, to):
-        here = tok_rows(last_z if way else 0, 1 - x, keep, rows - keep)
+        here = tok_rows(last_z if way else 0, 1 - x, keep_t, rows - keep_t)
         return remote(here, here, g_snd.at[way], g_rcv.at[way], to)
 
     def from_origin(way):
@@ -361,19 +361,18 @@
 
         @pl.when(inside(source))
         def _():
-            if True:
-                if h > 0:
-                    tok_z_arrived(way, h, part)
-                elif part == 0:
-                    absorb(way, source, x)
-                else:
-                    first_normed(way, (source, x)).wait_recv()
-                if h < nz - 2:
-                    @pl.when(inside(z + step))
-                    def _():
-                        tok_z(way, h + 1, part).start()
-
-                send_x(source, part)
+            if h > 0:
+                tok_z_arrived(way, h, part)
+            elif part == 0:
+                absorb(way, source, x)
+            else:
+                first_normed(way, (source, x)).wait_recv()
+            if h < nz - 2:
+                @pl.when(inside(z + step))
+                def _():
+                    tok_z(way, h + 1, part).start()
+
+            send_x(source, part)
 
     def pair_of(j):
         return z + ((j + 1) // 2) * (1 - 2 * (j % 2))
@@ -386,15 +385,14 @@
         gates[here, :] = jnp.dot(tok[here, :], wg[...], preferred_element_type=F32)
 
     def other_x_arrived(zz):
-        if True:
-            @pl.when(middle(zz))
-            def _():
-                whole = tok_rows(zz, 1 - x)
-                remote(whole, whole, x_snd.at[zz], x_rcv.at[zz], x_peer).wait_recv()
-
-            @pl.when(jnp.logical_not(middle(zz)))
-            def _():
-                tok_x_end(zz, 1 - x).wait_recv()
+        @pl.when(middle(zz))
+        def _():
+            whole = tok_rows(zz, 1 - x)
+            remote(whole, whole, x_snd.at[zz], x_rcv.at[zz], x_peer).wait_recv()
+
+        @pl.when(jnp.logical_not(middle(zz)))
+        def _():
+            tok_x_end(zz, 1 - x).wait_recv()
 
     def gate_step(j, carry):
         zz = pair_of(j)
@@ -421,8 +419,7 @@
         for way in range(2):
             @pl.when(from_origin(way) == h + 1)
             def _():
-                if True:
-                    tok_half(way, x_peer).wait_recv()
+                tok_half(way, x_peer).wait_recv()
 
                 @pl.when(inside(z + 1 - 2 * way))
                 def _():
@@ -433,36 +430,26 @@
             hop(h, part, 1 - near_way)
             hop(h, part, near_way)
         if h == 0:
-            if True:
-                absorb(2, z, 1 - x)
-                first_normed(2, (z, 1 - x)).wait_recv()
-                for way in range(2):
-                    @pl.when(from_origin(way) == 0)
-                    def _():
-                        tok_half(way, z_device(z + 1 - 2 * way)).start()
+            absorb(2, z, 1 - x)
+            first_normed(2, (z, 1 - x)).wait_recv()
+            for way in range(2):
+                @pl.when(from_origin(way) == 0)
+                def _():
+                    tok_half(way, z_device(z + 1 - 2 * way)).start()
             relay_to((pieces_w + 1) // 2)
         elif h == 1:
-            if True:
-                relay_to(pieces_w - (pieces_w + 1) // 2)
-                weight_ready(0)
-            if True:
-                lax.fori_loop(0, 3, gate_step, 0)
+            relay_to(pieces_w - (pieces_w + 1) // 2)
+            weight_ready(0)
+            lax.fori_loop(0, 3, gate_step, 0)
             relay_to(1)
         else:
             relay_to(1)
-            if True:
-                lax.fori_loop(2 * h - 1, 2 * h + 1, gate_step, 0)
+            lax.fori_loop(2 * h - 1, 2 * h + 1, gate_step, 0)
         halves(h)
-    if True:
-        relay_to(len(relays))
-
-        @pl.when(jnp.logical_not(middle(z)))
-        def _():
-            zz = last_z - z
-            other_x_arrived(zz)
-            make_gate(zz)
-
-        weight_ready(1)
+    relay_to(len(relays))
+    near_ready(1)
+    for s in range(pieces_w - 1):
+        far_ready(1, s)
 
     def columns_of(chip):
         return lax.rem(i // 2 + chips - chip, chips)
@@ -534,8 +521,7 @@
     def relay_half(p, way):
         @pl.when(middle(z))
         def _():
-            if True:
-                finish_half(p, way)
+            finish_half(p, way)
 
     def own_half(p):
         for way in range(2):
@@ -550,19 +536,17 @@
 
         @pl.when(inside(zz))
         def _():
-            if True:
-                @pl.when(middle(zz))
-                def _():
-                    sum_x_whole(p, zz).wait_recv()
-
-                @pl.when(jnp.logical_not(middle(zz)))
-                def _():
-                    sum_x(p, zz, 0).wait_recv()
+            @pl.when(middle(zz))
+            def _():
+                sum_x_whole(p, zz).wait_recv()
+
+            @pl.when(jnp.logical_not(middle(zz)))
+            def _():
+                sum_x(p, zz, 0).wait_recv()
 
             @pl.when(more)
             def _():
-                if True:
-                    sum_z(p, way, zz, True).wait_recv()
+                sum_z(p, way, zz, True).wait_recv()
                 z_out[p, zz] = (
                     own_part[p, zz] + x_in[p, zz].astype(F32) + z_in[p, way, zz].astype(F32)
                 ).astype(BF16)
@@ -574,41 +558,77 @@
             sum_z(p, way, zz).start()
 
     near_ready(2)
-    lag = turns - 2
+    first_zz = z + (nz - 2) * (1 - 2 * near_way)
+
+    def upward_over(zz, shards):
+        total = None
+        for q in shards:
+            here = pl.ds(pl.multiple_of(q * depth, depth), depth)
+            part = jnp.dot(tok[both_rows(zz), here], wu[here, :], preferred_element_type=F32)
+            total = part if total is None else total + part
+        return total
+
+    def make_hidden(zz, upward):
+        here = both_rows(zz)
+        gate = gates[here, :]
+        hidden[here, :] = (gate / (1.0 + jnp.exp(-gate)) * upward).astype(BF16)
+
+    def first_sums(zz):
+        for p in range(cuts):
+            down(0, (p,), zz)
+            send_sums(p, zz)
+            send_halves((p,), zz)
+
+    @pl.when(inside(first_zz))
+    def _():
+        upper[...] = upward_over(first_zz, [partner] + [lax.rem(i + 2 * d, n_in) for d in range(chips)])
+
+    far_ready(1, pieces_w - 1)
+
+    @pl.when(inside(first_zz))
+    def _():
+        make_hidden(first_zz, upper[...] + upward_over(
+            first_zz, [lax.rem(partner + 2 * d, n_in) for d in range(1, chips)]))
+        first_sums(first_zz)
 
     def hidden_step(j, carry):
         _, zz = owner(j)
 
-        @pl.when(jnp.logical_and(j >= lag, jnp.logical_not(middle(z))))
-        def _():
-            for p in range(cuts):
-                finish(p, *owner(j - lag))
-
-        @pl.when(inside(zz))
-        def _():
-            here = both_rows(zz)
-            gate = gates[here, :]
-            upward = jnp.dot(tok[here, :], wu[...], preferred_element_type=F32)
-            hidden[here, :] = (gate / (1.0 + jnp.exp(-gate)) * upward).astype(BF16)
-            down(0, range(cuts), zz)
+        @pl.when(jnp.logical_and(j == 3, jnp.logical_not(middle(z))))
+        def _():
+            finish(0, near_way, first_zz)
+
+        @pl.when(jnp.logical_and(j == turns - 1, jnp.logical_not(middle(z))))
+        def _():
+            for p in range(1, cuts):
+                finish(p, near_way, first_zz)
+
+        @pl.when(jnp.logical_and(inside(zz), zz != first_zz))
+        def _():
+            @pl.when(j < 2)
+            def _():
+                other_x_arrived(zz)
+                make_gate(zz)
+
+            make_hidden(zz, jnp.dot(tok[both_rows(zz), :], wu[...], preferred_element_type=F32))
 
             @pl.when(j < turns - 1)
             def _():
-                for p in range(cuts):
-                    send_sums(p, zz)
-                send_halves(range(cuts), zz)
+                first_sums(zz)
+
+            @pl.when(j == turns - 1)
+            def _():
+                down(0, range(cuts), zz)
 
         return carry
 
-    if True:
-        lax.fori_loop(0, turns, hidden_step, 0)
+    lax.fori_loop(0, turns, hidden_step, 0)
 
     near_end = jnp.where(near_way == 0, last_z, 0)
 
     def finish_end(p):
-        if True:
-            relay_half(p, near_way)
-            finish(p, near_way, near_end)
+        relay_half(p, near_way)
+        finish(p, near_way, near_end)
 
     def finish_way(p, way, skip):
         def step(n, carry):
@@ -622,26 +642,16 @@
 
         lax.fori_loop(0, nz - 1, step, 0)
 
-    def finish_middle(ps):
-        for p in ps:
-            if True:
-                relay_half(p, 1 - near_way)
-                finish_way(p, 1 - near_way, -1)
-            if True:
-                finish_way(p, near_way, near_end)
-
     def finish_outer(ps, start):
         def step(n, carry):
-            if True:
-                for p in ps:
-                    finish(p, near_way, z + (nz - 1 - n) * (1 - 2 * near_way))
+            for p in ps:
+                finish(p, near_way, z + (nz - 1 - n) * (1 - 2 * near_way))
             return carry
 
         lax.fori_loop(start, nz - 1, step, 0)
 
-    def far_down(s):
-        if True:
-            far_ready(2, s)
+    def far_down(s, hold=False):
+        far_ready(2, s)
 
         def step(t, carry):
             chip = 1 + t // turns
@@ -652,15 +662,16 @@
             def _():
                 down(chip, (s,), zz)
 
-                @pl.when(j < turns - 1)
+                @pl.when(j < (turns - 3 if hold else turns - 1))
                 def _():
                     send_sums(chip * cuts + s, zz)
                     send_halves((chip * cuts + s,), zz)
 
             return carry
 
-        if True:
-            lax.fori_loop(0, (chips - 1) * turns, step, 0)
+        lax.fori_loop(0, (chips - 1) * turns, step, 0)
+
+    rest = [c * cuts + s for s in range(cuts) for c in range(1, chips)]
 
     def own_sums(ps):
         for p in ps:
@@ -669,21 +680,6 @@
             @pl.when(middle(z))
             def _():
                 sum_x(p, z, 1).start()
-
-    @pl.when(middle(z))
-    def _():
-        own_sums(range(cuts))
-        for p in range(cuts):
-            finish_end(p)
-        relay_weight(2, 0)
-        finish_middle((0,))
-
-    @pl.when(jnp.logical_not(middle(z)))
-    def _():
-        relay_weight(2, 0)
-        finish(0, near_way, z + (nz - 2) * (1 - 2 * near_way))
-
-    rest = [c * cuts + s for s in range(cuts) for c in range(1, chips)]
 
     def drain_first():
         for d in steps:
@@ -745,63 +741,74 @@
         others = z_out.at[p, pl.ds(0, nz - 1)]
         remote(others, others, rz_snd.at[p], rz_rcv.at[p, 0], x_peer).wait_send()
 
-    if True:
-        drain_first()
-    for s in range(cuts):
-        far_down(s)
-        if s == 0:
-            @pl.when(middle(z))
-            def _():
-                finish_middle(range(1, cuts))
-
-            @pl.when(jnp.logical_not(middle(z)))
-            def _():
-                for p in range(1, cuts):
-                    finish(p, near_way, z + (nz - 2) * (1 - 2 * near_way))
-                finish_outer(range(cuts), 2)
-
-        if s < cuts - 1:
-            relay_weight(2, s + 1)
-        else:
-            @pl.when(middle(z))
-            def _():
-                own_sums(range(cuts, parts_n))
-
-            @pl.when(jnp.logical_not(middle(z)))
-            def _():
-                own_sums(range(parts_n))
-        for c in range(1, chips):
-            finish_end(c * cuts + s)
-    if True:
-        for k in range(3):
-            drain_weights(k)
-
     @pl.when(middle(z))
     def _():
-        finish_middle(rest)
+        own_sums(range(cuts))
+        for p in range(cuts):
+            relay_half(p, near_way)
+        relay_weight(2, 0)
+        far_down(0)
+        for p in range(cuts):
+            relay_half(p, 1 - near_way)
+        for p in range(cuts):
+            finish_way(p, near_way, near_end)
+        for p in range(cuts):
+            finish(p, near_way, near_end)
+        for s in range(1, cuts):
+            relay_weight(2, s)
+            far_down(s)
+        own_sums(rest)
+        for p in range(cuts):
+            finish_way(p, 1 - near_way, -1)
+        for p in rest:
+            finish_end(p)
+        for p in rest:
+            relay_half(p, 1 - near_way)
+        for p in rest:
+            finish_way(p, 1 - near_way, -1)
+            finish_way(p, near_way, near_end)
 
     @pl.when(jnp.logical_not(middle(z)))
     def _():
+        finish(0, near_way, near_end)
+        relay_weight(2, 0)
+        for p in range(1, cuts):
+            finish(p, near_way, near_end)
+        far_down(0, True)
+        finish_outer((0,), 2)
+        for s in range(1, cuts):
+            relay_weight(2, s)
+            for c in range(1, chips):
+                finish_end(c * cuts + s - 1)
+            far_down(s, True)
+        for p in rest:
+            send_sums(p, z + 1 - 2 * near_way)
+        own_sums(range(parts_n))
+        for c in range(1, chips):
+            finish_end(c * cuts + cuts - 1)
+        if cuts > 1:
+            finish_outer(range(1, cuts), 2)
         finish_outer(rest, 1)
 
-    if True:
-        for p in range(parts_n):
-            own_half(p)
+    drain_first()
+    for k in range(3):
+        drain_weights(k)
     for p in range(parts_n):
-        if True:
-            for way in range(2):
-                @pl.when(inside(z - (1 - 2 * way)))
-                def _():
-                    sum_z(p, way, z, True).wait_recv()
-                    own_part[p, z] = own_part[p, z] + z_in[p, way, z].astype(F32)
-            sum_x_whole(p, z).wait_recv()
-            for q in range(2):
-                source = 2 * columns_of(p // cuts) + q
-                here = pl.ds(pl.multiple_of(source * width + (p % cuts) * cw, cw), cw)
-                cols = slice(q * cw, (q + 1) * cw)
-                out_ref[:, here] = (
-                    after[:, here].astype(F32)
-                    + (own_part[p, z, :, cols] + x_in[p, z, :, cols].astype(F32))).astype(BF16)
+        own_half(p)
+    for p in range(parts_n):
+        for way in range(2):
+            @pl.when(inside(z - (1 - 2 * way)))
+            def _():
+                sum_z(p, way, z, True).wait_recv()
+                own_part[p, z] = own_part[p, z] + z_in[p, way, z].astype(F32)
+        sum_x_whole(p, z).wait_recv()
+        for q in range(2):
+            source = 2 * columns_of(p // cuts) + q
+            here = pl.ds(pl.multiple_of(source * width + (p % cuts) * cw, cw), cw)
+            cols = slice(q * cw, (q + 1) * cw)
+            out_ref[:, here] = (
+                after[:, here].astype(F32)
+                + (own_part[p, z, :, cols] + x_in[p, z, :, cols].astype(F32))).astype(BF16)
         if p < parts_n - 1:
             drain_sums(p)
 
@@ -821,18 +828,20 @@
     vmem = pl.BlockSpec(memory_space=pltpu.VMEM)
     hbm = pl.BlockSpec(memory_space=pl.ANY)
     spl = max(cuts, pieces_w)
-    half = rows - rows // 2
+    keep = rows * KEEP // 128
+    half = rows - keep
     return pl.pallas_call(
-        functools.partial(layer_kernel, n_out, n_in, cuts, pieces_w, early),
+        functools.partial(layer_kernel, n_out, n_in, cuts, pieces_w, early, keep),
         out_shape=pltpu.VMEM(resid.shape, BF16),
-        in_specs=[pl.BlockSpec(memory_space=pltpu.SMEM)] + [hbm] * 8,
+        in_specs=[hbm] * 9,
         out_specs=vmem,
         scratch_shapes=[
+            pltpu.SMEM(piece_order.shape, jnp.int32),
             pltpu.VMEM(resid.shape, BF16),
             pltpu.VMEM(queries.shape, BF16),
             pltpu.VMEM(out_proj.shape, BF16),
             pltpu.VMEM((1, model), F32),
-            dma((4,)),
+            dma((5,)),
             pltpu.VMEM((2 * n_in * rows, keyvals.shape[1]), BF16),
             pltpu.VMEM((model, units), BF16),
             pltpu.VMEM((model, units), BF16),
@@ -843,6 +852,7 @@
             pltpu.VMEM((3, early, model), BF16),
             pltpu.VMEM((3, early, queries.shape[1]), BF16),
             pltpu.VMEM((n_out * rows, units), F32),
+            pltpu.VMEM((2 * rows, units), F32),
             pltpu.VMEM((n_out * rows, units), BF16),
             pltpu.VMEM((parts_n, nz, rows, 2 * cw), BF16),
             pltpu.VMEM((parts_n, nz, rows, 2 * cw), BF16),

time: 99.1 us -> 96.1 us (0.970)
  Pallas kernels: 98.2 us -> 95.2 us
    pallas_call x1, Pallas kernels: 98.2 us -> 95.2 us  [per_device(): pl.pallas_call(functools.partial(layer_kernel, n_out, n_in, cuts, pieces_...]
where the time goes in v4:
time: 96.1 us; the launch traced here: 96 us
  Pallas kernels  95.2 us (99%)
    pallas_call x1, Pallas kernels, per_device(): pl.pallas_call(functools.partial(layer_kernel, n_out, n_in, cuts, pieces_...  95.2 us

profile of v4, /device:TPU:0, one launch (start us, length us, event | category | flops | bytes accessed | tf_op | source)
XLA Modules:
  0.0 96.0 jit_solution(15418183747699441576)
XLA Ops:
  0.0 95.2 %layer.1 = bf16[128,2048]{1,0:T(8,128)(2,1)S(1)} custom-call(s32[8]{0:T(128)} %order_hbm.1, bf16[128,2048]{1,0:T(8,128)(2,1)} %resid_hbm.1, bf16[128,256]{1,0:T(8,128)(2,1)} %query_hbm.1, bf16[128,256]{1,0:T(8,128)(2,1)} %kv_ref.1, bf16[256,2048]{1,0:T(8,128)(2,1)} %proj_hbm.1, f32[1,2048]{1,0:T(1,128)} %bitcast.1, bf16[512,896]{1,0:T(8,128)(2,1)} %wg_ref.1, ...), custom_call_target="tpu_custom_call" | custom-call | tf_op jit(solution)/shard_map/layer/pallas_call | solution.py:833
  95.2 0.8 copy.11

commit v5 on v4

--- a/solution.py
+++ b/solution.py
@@ -156,7 +156,7 @@
         if k == 2:
             return wd.at[q, s]
         full = wg if k == 0 else wu
-        size = depth // pieces_w
+        size = depth // pieces_w[k]
         return full.at[pl.ds(pl.multiple_of(q * depth + s * size, size), size)]
 
     srcs = (wg_ref, wu_ref, wd_ref)
@@ -164,11 +164,14 @@
     def w_src(k, s):
         if k == 2:
             return wd_ref.at[:, pl.ds(s * cw, cw)]
-        size = depth // pieces_w
+        size = depth // pieces_w[k]
         return srcs[k].at[pl.ds(s * size, size)]
 
     def w_parts(k):
-        return cuts if k == 2 else pieces_w
+        return pieces_w[k]
+
+    def w_index(k, s):
+        return sum(pieces_w[:k]) + s
 
     def shard(k, q):
         if k == 2:
@@ -180,12 +183,12 @@
         return lax.rem(i + n_in - 2 * d, n_in)
 
     def w_far(k, d, s):
-        return remote(w_src(k, s), slot(k, i, s), w_snd.at[k, d], w_rcv.at[k, d - 1, 0, s],
+        return remote(w_src(k, s), slot(k, i, s), w_snd.at[k, d], w_rcv.at[d - 1, 0, w_index(k, s)],
                       (o, lax.rem(i + 2 * d, n_in)))
 
     def w_relay(k, d, s):
         here = slot(k, far(d), s)
-        return remote(here, here, w_relay_snd.at[k, d], w_rcv.at[k, d - 1, 1, s], core_peer)
+        return remote(here, here, w_relay_snd.at[k, d], w_rcv.at[d - 1, 1, w_index(k, s)], core_peer)
 
     def w_pair(k, s):
         return remote(w_src(k, s), slot(k, i, s), w_pair_snd.at[k], w_pair_rcv.at[k], core_peer)
@@ -201,12 +204,12 @@
     def far_ready(k, s):
         for d in steps:
             here = slot(k, lax.rem(partner + n_in - 2 * d, n_in), s)
-            remote(here, here, w_relay_snd.at[k, d], w_rcv.at[k, d - 1, 1, s], core_peer).wait_recv()
+            remote(here, here, w_relay_snd.at[k, d], w_rcv.at[d - 1, 1, w_index(k, s)], core_peer).wait_recv()
 
     def relay_weight(k, s):
         for d in steps:
             here = slot(k, far(d), s)
-            remote(here, here, w_relay_snd.at[k, d], w_rcv.at[k, d - 1, 0, s], core_peer).wait_recv()
+            remote(here, here, w_relay_snd.at[k, d], w_rcv.at[d - 1, 0, w_index(k, s)], core_peer).wait_recv()
             w_relay(k, d, s).start()
 
     def weight_ready(k):
@@ -407,7 +410,17 @@
 
         return carry
 
-    relays = [(k, s) for k in range(2) for s in range(pieces_w)]
+    first_zz = z + (nz - 2) * (1 - 2 * near_way)
+
+    def upward_over(zz, shards):
+        total = None
+        for q in shards:
+            here = pl.ds(pl.multiple_of(q * depth, depth), depth)
+            part = jnp.dot(tok[both_rows(zz), here], wu[here, :], preferred_element_type=F32)
+            total = part if total is None else total + part
+        return total
+
+    relays = [(k, s) for k in range(2) for s in range(pieces_w[k])]
 
     def relay_to(n):
         while relays and n > 0:
@@ -436,20 +449,25 @@
                 @pl.when(from_origin(way) == 0)
                 def _():
                     tok_half(way, z_device(z + 1 - 2 * way)).start()
-            relay_to((pieces_w + 1) // 2)
+            relay_to((pieces_w[0] + 1) // 2)
         elif h == 1:
-            relay_to(pieces_w - (pieces_w + 1) // 2)
+            relay_to(pieces_w[0] // 2)
             weight_ready(0)
             lax.fori_loop(0, 3, gate_step, 0)
-            relay_to(1)
+            relay_to((pieces_w[1] + 3) // 4)
         else:
-            relay_to(1)
+            relay_to((pieces_w[1] + 7) // 8)
             lax.fori_loop(2 * h - 1, 2 * h + 1, gate_step, 0)
+        if h == nz - 2:
+            relay_to(len(relays) - 1)
+            near_ready(1)
+
+            @pl.when(inside(first_zz))
+            def _():
+                upper[...] = upward_over(first_zz, [i, partner])
+
         halves(h)
     relay_to(len(relays))
-    near_ready(1)
-    for s in range(pieces_w - 1):
-        far_ready(1, s)
 
     def columns_of(chip):
         return lax.rem(i // 2 + chips - chip, chips)
@@ -558,16 +576,6 @@
             sum_z(p, way, zz).start()
 
     near_ready(2)
-    first_zz = z + (nz - 2) * (1 - 2 * near_way)
-
-    def upward_over(zz, shards):
-        total = None
-        for q in shards:
-            here = pl.ds(pl.multiple_of(q * depth, depth), depth)
-            part = jnp.dot(tok[both_rows(zz), here], wu[here, :], preferred_element_type=F32)
-            total = part if total is None else total + part
-        return total
-
     def make_hidden(zz, upward):
         here = both_rows(zz)
         gate = gates[here, :]
@@ -581,14 +589,15 @@
 
     @pl.when(inside(first_zz))
     def _():
-        upper[...] = upward_over(first_zz, [partner] + [lax.rem(i + 2 * d, n_in) for d in range(chips)])
-
-    far_ready(1, pieces_w - 1)
+        upper[...] += upward_over(first_zz, [lax.rem(i + 2 * d, n_in) for d in steps])
+
+    for s in range(pieces_w[1]):
+        far_ready(1, s)
 
     @pl.when(inside(first_zz))
     def _():
         make_hidden(first_zz, upper[...] + upward_over(
-            first_zz, [lax.rem(partner + 2 * d, n_in) for d in range(1, chips)]))
+            first_zz, [lax.rem(partner + 2 * d, n_in) for d in steps]))
         first_sums(first_zz)
 
     def hidden_step(j, carry):
@@ -820,14 +829,13 @@
     units, width = w_down.shape
     nz, chips = n_out // 2, n_in // 2
     cuts = max(1, width // 256)
-    pieces_w = max(1, 16 // n_in)
+    pieces_w = (max(1, 8 // n_in), max(1, 32 // n_in), cuts)
     cw = width // cuts
     parts_n = chips * cuts
     early = rows * 3 // 4
     dma = pltpu.SemaphoreType.DMA
     vmem = pl.BlockSpec(memory_space=pltpu.VMEM)
     hbm = pl.BlockSpec(memory_space=pl.ANY)
-    spl = max(cuts, pieces_w)
     keep = rows * KEEP // 128
     half = rows - keep
     return pl.pallas_call(
@@ -864,7 +872,7 @@
             pltpu.VMEM((parts_n, 2, half, 2 * cw), BF16),
             dma(()), dma((2, chips)), dma((2, chips)), dma((2, n_in)),
             dma((3,)), dma((3,)), dma((3,)), dma((3, chips)), dma((3, chips)),
-            dma((3, max(chips - 1, 1), 2, spl)),
+            dma((chips - 1, 2, sum(pieces_w))),
             dma((3,)), dma((3,)), dma((3,)), dma((3,)), dma((3,)),
             dma((2, nz - 2)), dma((2, 2, nz - 2)), dma((2,)), dma((2,)), dma((nz,)), dma((nz,)),
             dma((2, parts_n)), dma((parts_n, nz)), dma((parts_n,)), dma((parts_n, nz + 1)),

time: 96.1 us -> 95.7 us (level)
  no operation moved by 1% of the time
where the time goes in v5:
time: 95.7 us; the launch traced here: 95.5 us
  Pallas kernels  94.7 us (99%)
    pallas_call x1, Pallas kernels, per_device(): pl.pallas_call(functools.partial(layer_kernel, n_out, n_in, cuts, pieces_...  94.7 us

profile of v5, /device:TPU:0, one launch (start us, length us, event | category | flops | bytes accessed | tf_op | source)
XLA Modules:
  0.0 95.5 jit_solution(11843129131812527477)
XLA Ops:
  0.0 94.7 %layer.1 = bf16[128,2048]{1,0:T(8,128)(2,1)S(1)} custom-call(s32[8]{0:T(128)} %order_hbm.1, bf16[128,2048]{1,0:T(8,128)(2,1)} %resid_hbm.1, bf16[128,256]{1,0:T(8,128)(2,1)} %query_hbm.1, bf16[128,256]{1,0:T(8,128)(2,1)} %kv_ref.1, bf16[256,2048]{1,0:T(8,128)(2,1)} %proj_hbm.1, f32[1,2048]{1,0:T(1,128)} %bitcast.1, bf16[512,896]{1,0:T(8,128)(2,1)} %wg_ref.1, ...), custom_call_target="tpu_custom_call" | custom-call | tf_op jit(solution)/shard_map/layer/pallas_call | solution.py:841
  94.7 0.8 copy.11

commit v6 on v5

--- a/solution.py
+++ b/solution.py
@@ -183,12 +183,12 @@
         return lax.rem(i + n_in - 2 * d, n_in)
 
     def w_far(k, d, s):
-        return remote(w_src(k, s), slot(k, i, s), w_snd.at[k, d], w_rcv.at[d - 1, 0, w_index(k, s)],
+        return remote(w_src(k, s), slot(k, i, s), w_snd.at[k, d - 1], w_rcv.at[d - 1, 0, w_index(k, s)],
                       (o, lax.rem(i + 2 * d, n_in)))
 
     def w_relay(k, d, s):
         here = slot(k, far(d), s)
-        return remote(here, here, w_relay_snd.at[k, d], w_rcv.at[d - 1, 1, w_index(k, s)], core_peer)
+        return remote(here, here, w_relay_snd.at[k, d - 1], w_rcv.at[d - 1, 1, w_index(k, s)], core_peer)
 
     def w_pair(k, s):
         return remote(w_src(k, s), slot(k, i, s), w_pair_snd.at[k], w_pair_rcv.at[k], core_peer)
@@ -204,12 +204,12 @@
     def far_ready(k, s):
         for d in steps:
             here = slot(k, lax.rem(partner + n_in - 2 * d, n_in), s)
-            remote(here, here, w_relay_snd.at[k, d], w_rcv.at[d - 1, 1, w_index(k, s)], core_peer).wait_recv()
+            remote(here, here, w_relay_snd.at[k, d - 1], w_rcv.at[d - 1, 1, w_index(k, s)], core_peer).wait_recv()
 
     def relay_weight(k, s):
         for d in steps:
             here = slot(k, far(d), s)
-            remote(here, here, w_relay_snd.at[k, d], w_rcv.at[d - 1, 0, w_index(k, s)], core_peer).wait_recv()
+            remote(here, here, w_relay_snd.at[k, d - 1], w_rcv.at[d - 1, 0, w_index(k, s)], core_peer).wait_recv()
             w_relay(k, d, s).start()
 
     def weight_ready(k):
@@ -221,8 +221,8 @@
         mine = shard(k, i)
         remote(mine, mine, w_pair_snd.at[k], w_pair_rcv.at[k], core_peer).wait_send()
         for d in steps:
-            remote(mine, mine, w_snd.at[k, d], w_pair_rcv.at[k], core_peer).wait_send()
-            remote(mine, mine, w_relay_snd.at[k, d], w_pair_rcv.at[k], core_peer).wait_send()
+            remote(mine, mine, w_snd.at[k, d - 1], w_pair_rcv.at[k], core_peer).wait_send()
+            remote(mine, mine, w_relay_snd.at[k, d - 1], w_pair_rcv.at[k], core_peer).wait_send()
 
     for k in range(3):
         for s in range(w_parts(k)):
@@ -477,21 +477,21 @@
 
     def sum_x(p, zz, part):
         there = pl.ds(part * keep, rows - keep if part else keep)
-        return remote(x_out.at[p, zz, there], x_in.at[p, zz, there], rx_snd.at[part, p],
+        return remote(x_out.at[p, zz, there], x_in.at[p, zz, there], rx_snd.at[part],
                       rx_rcv.at[p, zz], x_peer)
 
     def sum_x_whole(p, zz):
-        return remote(x_out.at[p, zz], x_in.at[p, zz], rx_snd.at[0, p], rx_rcv.at[p, zz], x_peer)
+        return remote(x_out.at[p, zz], x_in.at[p, zz], rx_snd.at[0], rx_rcv.at[p, zz], x_peer)
 
     def sum_z(p, way, zz, here=False):
         step = jnp.where(inside(z + 1 - 2 * way), 1 - 2 * way, 0)
         off = 0 if here else step
-        return remote(z_out.at[p, zz], z_in.at[p, way, zz], rz_snd.at[p],
+        return remote(z_out.at[p, zz], z_in.at[p, way, zz], rz_snd,
                       rz_rcv.at[p, jnp.where(jnp.logical_and(way == 1, zz == z + off), nz, zz)],
                       z_device(z + step))
 
     def sum_half(p, way, to):
-        return remote(h_out.at[p, way], h_in.at[p, way], rh_snd.at[p, way], rh_rcv.at[p, way], to)
+        return remote(h_out.at[p, way], h_in.at[p, way], rh_snd.at[way], rh_rcv.at[p, way], to)
 
     def next_z(way):
         return z_device(jnp.clip(z + 1 - 2 * way, 0, last_z))
@@ -591,14 +591,38 @@
     def _():
         upper[...] += upward_over(first_zz, [lax.rem(i + 2 * d, n_in) for d in steps])
 
+    @pl.when(jnp.logical_and(jnp.logical_not(middle(z)), core == 1))
+    def _():
+        other_x_arrived(last_z - z)
+        make_gate(last_z - z)
+
     for s in range(pieces_w[1]):
         far_ready(1, s)
 
     @pl.when(inside(first_zz))
     def _():
-        make_hidden(first_zz, upper[...] + upward_over(
-            first_zz, [lax.rem(partner + 2 * d, n_in) for d in steps]))
-        first_sums(first_zz)
+        for xx in (1 - x, x):
+            here = pl.ds(pl.multiple_of((first_zz * 2 + xx) * rows, rows), rows)
+            upward = upper[pl.ds(pl.multiple_of(xx * rows, rows), rows), :]
+            for d in steps:
+                q = lax.rem(partner + 2 * d, n_in)
+                there = pl.ds(pl.multiple_of(q * depth, depth), depth)
+                upward += jnp.dot(tok[here, there], wu[there, :], preferred_element_type=F32)
+            gate = gates[here, :]
+            hidden[here, :] = (gate / (1.0 + jnp.exp(-gate)) * upward).astype(BF16)
+            for q in range(2):
+                part = jnp.dot(hidden[here, :], wd[2 * columns_of(0) + q, 0], preferred_element_type=F32)
+                cols = slice(q * cw, (q + 1) * cw)
+                if xx is x:
+                    own_part[0, first_zz, :, cols] = part
+                else:
+                    x_out[0, first_zz, :, cols] = part.astype(BF16)
+                    h_own[0, jnp.where(middle(first_zz), 2, end_way(first_zz)), :, cols] = part[keep:]
+            if xx is not x:
+                send_sums(0, first_zz)
+        for p in range(1, cuts):
+            down(0, (p,), first_zz)
+            send_sums(p, first_zz)
 
     def hidden_step(j, carry):
         _, zz = owner(j)
@@ -614,7 +638,7 @@
 
         @pl.when(jnp.logical_and(inside(zz), zz != first_zz))
         def _():
-            @pl.when(j < 2)
+            @pl.when(jnp.logical_and(j < 2, core == 0))
             def _():
                 other_x_arrived(zz)
                 make_gate(zz)
@@ -733,22 +757,23 @@
                     whole = tok_rows(zz, x)
                     remote(whole, whole, x_snd.at[zz], x_rcv.at[zz], x_peer).wait_send()
 
-    def drain_sums(p):
+    def drain_sums():
         for way in range(2):
             @pl.when(inside(z + 1 - 2 * way))
             def _():
-                sum_half(p, way, x_peer).wait_send()
-        first = x_out.at[p, :, pl.ds(0, keep)]
-        remote(first, first, rx_snd.at[0, p], rx_rcv.at[p, 0], x_peer).wait_send()
+                halves_out = h_out.at[:, way]
+                remote(halves_out, halves_out, rh_snd.at[way], rh_rcv.at[0, way], x_peer).wait_send()
+        first = x_out.at[:, :, pl.ds(0, keep)]
+        remote(first, first, rx_snd.at[0], rx_rcv.at[0, 0], x_peer).wait_send()
 
         def second(n):
-            there = x_out.at[p, pl.ds(0, n), pl.ds(keep, rows - keep)]
-            remote(there, there, rx_snd.at[1, p], rx_rcv.at[p, 0], x_peer).wait_send()
+            there = x_out.at[:, pl.ds(0, n), pl.ds(keep, rows - keep)]
+            remote(there, there, rx_snd.at[1], rx_rcv.at[0, 0], x_peer).wait_send()
 
         pl.when(middle(z))(lambda: second(nz - 2))
         pl.when(jnp.logical_not(middle(z)))(lambda: second(nz - 1))
-        others = z_out.at[p, pl.ds(0, nz - 1)]
-        remote(others, others, rz_snd.at[p], rz_rcv.at[p, 0], x_peer).wait_send()
+        others = z_out.at[:, pl.ds(0, nz - 1)]
+        remote(others, others, rz_snd, rz_rcv.at[0, 0], x_peer).wait_send()
 
     @pl.when(middle(z))
     def _():
@@ -818,10 +843,8 @@
             out_ref[:, here] = (
                 after[:, here].astype(F32)
                 + (own_part[p, z, :, cols] + x_in[p, z, :, cols].astype(F32))).astype(BF16)
-        if p < parts_n - 1:
-            drain_sums(p)
-
-    drain_sums(parts_n - 1)
+
+    drain_sums()
 
 
 def per_device(n_out, n_in, resid, queries, keyvals, piece_order, out_proj, mlp_gain, w_gate, w_up, w_down):
@@ -871,12 +894,12 @@
             pltpu.VMEM((parts_n, 2, half, 2 * cw), BF16),
             pltpu.VMEM((parts_n, 2, half, 2 * cw), BF16),
             dma(()), dma((2, chips)), dma((2, chips)), dma((2, n_in)),
-            dma((3,)), dma((3,)), dma((3,)), dma((3, chips)), dma((3, chips)),
+            dma((3,)), dma((3,)), dma((3,)), dma((3, chips - 1)), dma((3, chips - 1)),
             dma((chips - 1, 2, sum(pieces_w))),
             dma((3,)), dma((3,)), dma((3,)), dma((3,)), dma((3,)),
             dma((2, nz - 2)), dma((2, 2, nz - 2)), dma((2,)), dma((2,)), dma((nz,)), dma((nz,)),
-            dma((2, parts_n)), dma((parts_n, nz)), dma((parts_n,)), dma((parts_n, nz + 1)),
-            dma((parts_n, 2)), dma((parts_n, 2)),
+            dma((2,)), dma((parts_n, nz)), dma(()), dma((parts_n, nz + 1)),
+            dma((2,)), dma((parts_n, 2)),
         ],
         compiler_params=pltpu.CompilerParams(
             collective_id=0, has_side_effects=True, vmem_limit_bytes=63000 * 1024

time: 95.7 us -> 95.1 us (level)
  no operation moved by 1% of the time
where the time goes in v6:
time: 95.1 us; the launch traced here: 94.9 us
  Pallas kernels  94.1 us (99%)
    pallas_call x1, Pallas kernels, per_device(): pl.pallas_call(functools.partial(layer_kernel, n_out, n_in, cuts, pieces_...  94.1 us

profile of v6, /device:TPU:0, one launch (start us, length us, event | category | flops | bytes accessed | tf_op | source)
XLA Modules:
  0.0 94.9 jit_solution(11240761075293439427)
XLA Ops:
  0.0 94.1 %layer.1 = bf16[128,2048]{1,0:T(8,128)(2,1)S(1)} custom-call(s32[8]{0:T(128)} %order_hbm.1, bf16[128,2048]{1,0:T(8,128)(2,1)} %resid_hbm.1, bf16[128,256]{1,0:T(8,128)(2,1)} %query_hbm.1, bf16[128,256]{1,0:T(8,128)(2,1)} %kv_ref.1, bf16[256,2048]{1,0:T(8,128)(2,1)} %proj_hbm.1, f32[1,2048]{1,0:T(1,128)} %bitcast.1, bf16[512,896]{1,0:T(8,128)(2,1)} %wg_ref.1, ...), custom_call_target="tpu_custom_call" | custom-call | tf_op jit(solution)/shard_map/layer/pallas_call | solution.py:864
  94.1 0.8 copy.11

commit v7 on v6

--- a/solution.py
+++ b/solution.py
@@ -131,17 +131,17 @@
             return x_peer if link == 2 else z_device(z + 1 - 2 * link)
         return z_device(z + 1 - 2 * link)
 
-    def first_resid(link):
+    def first_resid(link, to=None):
         return remote(resid_hbm.at[pl.ds(0, early)], res_in.at[link], r_snd.at[link], r_rcv.at[link],
-                      target(link))
-
-    def first_attended(link):
+                      to or target(link))
+
+    def first_attended(link, to=None):
         return remote(att_own.at[pl.ds(0, early)], att_in.at[link], a_snd.at[link], a_rcv.at[link],
-                      target(link))
-
-    def first_normed(link, source=None):
+                      to or target(link))
+
+    def first_normed(link, source=None, to=None):
         here = tok_rows(*(source or (z, x)), early, rows - early)
-        return remote(here, here, r_snd.at[link], n_rcv.at[link], target(link))
+        return remote(here, here, r_snd.at[link], n_rcv.at[link], to or target(link))
 
     def send_link(link, act):
         if link == 2:
@@ -354,8 +354,8 @@
     near_way = jnp.where(2 * z < nz, 0, 1)
 
     def absorb(link, zz, xx):
-        first_resid(link).wait_recv()
-        first_attended(link).wait_recv()
+        first_resid(link, x_peer).wait_recv()
+        first_attended(link, x_peer).wait_recv()
         tok_rows(zz, xx, 0, early)[...] = normed_of(res_in[link], att_in[link])[1]
 
     def hop(h, part, way):
@@ -369,7 +369,7 @@
             elif part == 0:
                 absorb(way, source, x)
             else:
-                first_normed(way, (source, x)).wait_recv()
+                first_normed(way, (source, x), x_peer).wait_recv()
             if h < nz - 2:
                 @pl.when(inside(z + step))
                 def _():
@@ -444,7 +444,7 @@
             hop(h, part, near_way)
         if h == 0:
             absorb(2, z, 1 - x)
-            first_normed(2, (z, 1 - x)).wait_recv()
+            first_normed(2, (z, 1 - x), x_peer).wait_recv()
             for way in range(2):
                 @pl.when(from_origin(way) == 0)
                 def _():

time: 95.1 us -> 95.1 us (level)
  no operation moved by 1% of the time
where the time goes in v7:
time: 95.1 us; the launch traced here: 94.9 us
  Pallas kernels  94.1 us (99%)
    pallas_call x1, Pallas kernels, per_device(): pl.pallas_call(functools.partial(layer_kernel, n_out, n_in, cuts, pieces_...  94.1 us

profile of v7, /device:TPU:0, one launch (start us, length us, event | category | flops | bytes accessed | tf_op | source)
XLA Modules:
  0.0 94.9 jit_solution(11240761075293439427)
XLA Ops:
  0.0 94.1 %layer.1 = bf16[128,2048]{1,0:T(8,128)(2,1)S(1)} custom-call(s32[8]{0:T(128)} %order_hbm.1, bf16[128,2048]{1,0:T(8,128)(2,1)} %resid_hbm.1, bf16[128,256]{1,0:T(8,128)(2,1)} %query_hbm.1, bf16[128,256]{1,0:T(8,128)(2,1)} %kv_ref.1, bf16[256,2048]{1,0:T(8,128)(2,1)} %proj_hbm.1, f32[1,2048]{1,0:T(1,128)} %bitcast.1, bf16[512,896]{1,0:T(8,128)(2,1)} %wg_ref.1, ...), custom_call_target="tpu_custom_call" | custom-call | tf_op jit(solution)/shard_map/layer/pallas_call | solution.py:864
  94.1 0.8 copy.11

commit v8 on v7

--- a/solution.py
+++ b/solution.py
@@ -224,10 +224,13 @@
             remote(mine, mine, w_snd.at[k, d - 1], w_pair_rcv.at[k], core_peer).wait_send()
             remote(mine, mine, w_relay_snd.at[k, d - 1], w_pair_rcv.at[k], core_peer).wait_send()
 
-    for k in range(3):
+    def send_far(k):
         for s in range(w_parts(k)):
             for d in steps:
                 w_far(k, d, s).start()
+
+    send_far(0)
+    send_far(1)
     for k in range(3):
         for s in range(w_parts(k)):
             w_pair(k, s).start()
@@ -460,6 +463,7 @@
             lax.fori_loop(2 * h - 1, 2 * h + 1, gate_step, 0)
         if h == nz - 2:
             relay_to(len(relays) - 1)
+            send_far(2)
             near_ready(1)
 
             @pl.when(inside(first_zz))
@@ -855,7 +859,7 @@
     pieces_w = (max(1, 8 // n_in), max(1, 32 // n_in), cuts)
     cw = width // cuts
     parts_n = chips * cuts
-    early = rows * 3 // 4
+    early = rows * 80 // 128
     dma = pltpu.SemaphoreType.DMA
     vmem = pl.BlockSpec(memory_space=pltpu.VMEM)
     hbm = pl.BlockSpec(memory_space=pl.ANY)

time: 95.1 us -> 94.7 us (level)
  no operation moved by 1% of the time
where the time goes in v8:
time: 94.7 us; the launch traced here: 94.5 us
  Pallas kernels  93.7 us (99%)
    pallas_call x1, Pallas kernels, per_device(): pl.pallas_call(functools.partial(layer_kernel, n_out, n_in, cuts, pieces_...  93.7 us

profile of v8, /device:TPU:0, one launch (start us, length us, event | category | flops | bytes accessed | tf_op | source)
XLA Modules:
  0.0 94.5 jit_solution(4486696418315346258)
XLA Ops:
  0.0 93.7 %layer.1 = bf16[128,2048]{1,0:T(8,128)(2,1)S(1)} custom-call(s32[8]{0:T(128)} %order_hbm.1, bf16[128,2048]{1,0:T(8,128)(2,1)} %resid_hbm.1, bf16[128,256]{1,0:T(8,128)(2,1)} %query_hbm.1, bf16[128,256]{1,0:T(8,128)(2,1)} %kv_ref.1, bf16[256,2048]{1,0:T(8,128)(2,1)} %proj_hbm.1, f32[1,2048]{1,0:T(1,128)} %bitcast.1, bf16[512,896]{1,0:T(8,128)(2,1)} %wg_ref.1, ...), custom_call_target="tpu_custom_call" | custom-call | tf_op jit(solution)/shard_map/layer/pallas_call | solution.py:868
  93.7 0.8 copy.11
